TPU v7x, 256 devices: a whole 4x4x8 slice. The times are simulated.
256 devices in a mesh: frow: 8 (over y, x_lo), fcol: 32 (over z, x_hi, core).
Axes of the slice: x: 4 (x_hi: 2, x_lo: 2; x = x_hi * 2 + x_lo), y: 4, z: 8, core: 2. Of those that a mesh axis runs over, the one named last changes fastest.
Arguments:
- science: float32 [4, 1024, 4096], P(None, 'frow', 'fcol')
- pixel_mask: int32 [4, 1024, 4096], P(None, 'frow', 'fcol'), may hold values from 0 to 3, as said below
- coadd_image: float32 [1024, 4096], P('frow', 'fcol')
- coadd_variance: float32 [1024, 4096], P('frow', 'fcol'), may hold values from 0.5 to 2
- dither: int32 [4, 2], replicated, may hold values from -113 to 113, as said below
- stamps: int32 [4, 8, 32, 12], P(None, 'frow', 'fcol'), may hold values from -1 to 15, as said below
Outputs:
- scaled_difference: float32 [4, 1024, 4096], P(None, 'frow', 'fcol')
Inputs may be any that keep to these rules, and one draw needn't show every extreme that they name: `pixel_mask`: 0 marks a usable pixel; 1 a bad one, 2 a saturated one, 3 both. dither[v, 0] is the row offset and dither[v, 1] the column offset of visit v. `stamps`: cell numbers, row-major over the (4) x (4) cells of the tile; distinct within a tile and visit; live entries first, then -1; at least 4 live entries, and every visit has a tile with all 12 live.
All inputs are finite; a program needn't handle non-finite values.
Results may differ from a plain program's by a relative error of at most 0.023.
Values sent between devices are 32-bit elements; how exact they have to be, the bound alone decides.
No kernel may reach another device: no remote copies, remote signals or barrier semaphores. Data moves between devices by JAX's collectives and lax.ppermute only.
A program may use at most 128 MiB of HBM per device.

v0:
```python
import jax
import jax.numpy as jnp
from jax import lax
from jax.sharding import PartitionSpec as P

V = 4
TH = 128
TW = 128
R = 15
NB = 30
STAMP = 32
DMAX = 113


SPREADS = (0.75, 1.5, 3.0)


def with_halo(block, sides, width):
    for axis, dim in sides:
        count = lax.axis_size(axis)
        forward = [(i, i + 1) for i in range(count - 1)]
        backward = [(target, source) for source, target in forward]
        low = lax.ppermute(
            lax.slice_in_dim(block, block.shape[dim] - width, None, axis=dim), axis, forward
        )
        high = lax.ppermute(lax.slice_in_dim(block, 0, width, axis=dim), axis, backward)
        block = jnp.concatenate([low, block, high], axis=dim)
    return block


def kernel_table(radius):
    offsets = jnp.arange(-radius, radius + 1, dtype=jnp.float32)
    profiles = []
    for spread in SPREADS:
        for degree in range(4):
            profile = (
                jnp.exp(-offsets * offsets / (2.0 * spread * spread)) * (offsets / spread) ** degree
            )
            profiles.append(profile / jnp.sqrt(jnp.sum(profile * profile)))
    return jnp.stack(profiles).astype(jnp.bfloat16)


def basis_pairs():
    along_rows = []
    along_cols = []
    for family in range(3):
        for row_degree in range(4):
            for col_degree in range(4 - row_degree):
                along_rows.append(family * 4 + row_degree)
                along_cols.append(family * 4 + col_degree)
    return (along_rows, along_cols)


def solve_fit(normal_matrix, normal_vector):
    unknowns = normal_matrix.shape[-1]
    trace_sum = jnp.einsum("fii->f", normal_matrix)
    ridge_term = 0.001 * trace_sum / unknowns
    shifted = normal_matrix + ridge_term[:, None, None] * jnp.eye(unknowns, dtype=jnp.float32)
    factor = jnp.linalg.cholesky(shifted)
    solved = jax.scipy.linalg.cho_solve((factor, True), normal_vector[..., None])[..., 0]
    return solved.reshape(normal_matrix.shape[0], 3, unknowns // 3)


def toeplitz_table(rows_out, table):
    tap_count = 2 * R + 1
    offsets = jnp.arange(rows_out + 2 * R)[None, :] - jnp.arange(rows_out)[:, None]
    inside = (offsets >= 0) & (offsets < tap_count)
    clipped = jnp.clip(offsets, 0, tap_count - 1)
    return jnp.where(inside[None], table[:, clipped], jnp.zeros((), jnp.bfloat16))


def on_device(science, pixel_mask, coadd_image, coadd_variance, dither, stamps):
    highest = lax.Precision.HIGHEST
    margin = DMAX + R
    planes = jnp.stack([coadd_image, coadd_variance])
    padded = with_halo(planes, (("frow", 1), ("fcol", 2)), margin)
    padded_image = padded[0].astype(jnp.bfloat16)
    padded_var = padded[1]
    table = kernel_table(R)
    along_rows, along_cols = basis_pairs()
    block_cols = min(128, TW)
    block_rows = min(128, TH)
    col_offsets = jnp.arange(block_cols + 2 * R)[:, None] - jnp.arange(block_cols)[None, :]
    col_inside = (col_offsets >= 0) & (col_offsets <= 2 * R)
    col_toeplitz = jnp.where(
        col_inside[None], table[:, jnp.clip(col_offsets, 0, 2 * R)], jnp.zeros((), jnp.bfloat16)
    )
    row_toeplitz = toeplitz_table(block_rows, table[jnp.array(along_rows)])
    column_choice = jnp.array(along_cols)
    cells_down = TH // STAMP
    cells_across = TW // STAMP
    cell_total = cells_down * cells_across
    half_rows = TH / 2.0
    half_cols = TW / 2.0
    row_coord = (jnp.arange(TH, dtype=jnp.float32) + 0.5 - half_rows) / half_rows
    col_coord = (jnp.arange(TW, dtype=jnp.float32) + 0.5 - half_cols) / half_cols
    row_flat = jnp.broadcast_to(row_coord[:, None], (TH, TW)).reshape(TH * TW)
    col_flat = jnp.broadcast_to(col_coord[None, :], (TH, TW)).reshape(TH * TW)
    cell_number = jnp.arange(cell_total, dtype=jnp.int32)
    cell_row = cell_number // cells_across
    cell_col = cell_number % cells_across
    centre_row = (cell_row * STAMP + STAMP / 2.0 - half_rows) / half_rows
    centre_col = (cell_col * STAMP + STAMP / 2.0 - half_cols) / half_cols
    spatial = jnp.stack([jnp.ones_like(centre_row), centre_col, centre_row]).astype(jnp.float32)

    def cell_planes(plane):
        return (
            plane.reshape(cells_down, STAMP, cells_across, STAMP)
            .transpose(0, 2, 1, 3)
            .reshape(cell_total, STAMP * STAMP)
        )

    basis_list = []
    var_windows = []
    usable_list = []
    normal_matrices = []
    normal_vectors = []
    for v in range(V):
        row_shift = dither[v, 0]
        col_shift = dither[v, 1]
        window = lax.dynamic_slice(
            padded_image, (DMAX + row_shift, DMAX + col_shift), (TH + 2 * R, TW + 2 * R)
        )
        pieces = jnp.stack([window], axis=1)
        column_pass = jnp.einsum(
            "hbj,fjx->fhbx", pieces, col_toeplitz, preferred_element_type=jnp.float32
        )
        column_pass = column_pass.astype(jnp.bfloat16).reshape(12, TH + 2 * R, TW)
        chosen = column_pass[column_choice]
        blocks = jnp.einsum(
            "kyj,kjx->kyx", row_toeplitz, chosen, preferred_element_type=jnp.float32
        ).astype(jnp.bfloat16)
        var_window = lax.dynamic_slice(
            padded_var, (margin + row_shift, margin + col_shift), (TH, TW)
        )
        usable = (pixel_mask[v] == 0).astype(jnp.float32)
        weight = usable / (0.25 + var_window)
        basis_cells = (
            blocks.reshape(NB, cells_down, STAMP, cells_across, STAMP)
            .transpose(1, 3, 0, 2, 4)
            .reshape(cell_total, NB, STAMP * STAMP)
        )
        ones_row = jnp.ones((cell_total, 1, STAMP * STAMP), jnp.bfloat16)
        design = jnp.concatenate([basis_cells, ones_row], axis=1)
        weighted = (design * cell_planes(weight)[:, None, :]).astype(jnp.bfloat16)
        gram_cells = jnp.einsum(
            "ckp,clp->ckl", weighted, design, preferred_element_type=jnp.float32
        )
        right_cells = jnp.einsum(
            "ckp,cp->ck",
            weighted,
            cell_planes(science[v]).astype(jnp.bfloat16),
            preferred_element_type=jnp.float32,
        )
        cell_list = stamps[v, 0, 0]
        cell_use = jnp.sum((cell_list[:, None] == cell_number[None, :]).astype(jnp.float32), axis=0)
        normal_matrix = jnp.einsum(
            "ac,bc,c,ckl->akbl", spatial, spatial, cell_use, gram_cells, precision=highest
        )
        normal_matrices.append(normal_matrix.reshape(3 * (NB + 1), 3 * (NB + 1)))
        normal_vectors.append(
            jnp.einsum("ac,c,ck->ak", spatial, cell_use, right_cells, precision=highest).reshape(
                3 * (NB + 1)
            )
        )
        basis_list.append(blocks)
        var_windows.append(var_window)
        usable_list.append(usable)
    all_coefficients = solve_fit(jnp.stack(normal_matrices), jnp.stack(normal_vectors))
    totals = []
    differences = []
    for v in range(V):
        coefficients = all_coefficients[v]
        coef_main = coefficients[:, :NB]
        coef_high = coef_main.astype(jnp.bfloat16)
        coef_low = (coef_main - coef_high.astype(jnp.float32)).astype(jnp.bfloat16)
        stacked = jnp.concatenate([coef_high, coef_low], axis=0)
        weighted_sums = jnp.dot(
            stacked, basis_list[v].reshape(NB, TH * TW), preferred_element_type=jnp.float32
        )
        combined = weighted_sums[:3] + weighted_sums[3:] + coefficients[:, NB : NB + 1]
        fitted_model = (combined[0] + col_flat * combined[1] + row_flat * combined[2]).reshape(
            TH, TW
        )
        difference = science[v] - fitted_model
        totals.append(jnp.sum(usable_list[v] * difference * difference))
        differences.append(difference)
    strip_totals = lax.psum(jnp.stack(totals), "fcol")
    pixel_count = TH * TW * lax.axis_size("fcol")
    scaled = [
        differences[v] * lax.rsqrt(strip_totals[v] / pixel_count + var_windows[v] + 1e-06)
        for v in range(V)
    ]
    return jnp.stack(scaled)


def solution(mesh):
    in_specs = (
        P(None, "frow", "fcol"),
        P(None, "frow", "fcol"),
        P("frow", "fcol"),
        P("frow", "fcol"),
        P(),
        P(None, "frow", "fcol", None),
    )
    out_specs = P(None, "frow", "fcol")
    return jax.shard_map(
        on_device, mesh=mesh, in_specs=in_specs, out_specs=out_specs, check_vma=False
    )
```

profile of v0, /device:TPU:24, one launch (start us, length us, event | category | flops | bytes accessed | tf_op | source)
XLA Modules:
  0.0 451.9 jit_solution(16221667498306995601)
XLA Ops:
  0.0 0.9 pad_maximum_fusion.3
  0.9 3.6 collective-permute-start.1
  4.5 2.3 collective-permute-start
  26.6 1.6 fusion.208
  28.5 1.0 fusion.207
  29.6 1.3 pad_clamp_fusion.2
  31.6 0.9 pad_maximum_fusion.1
  32.5 1.3 collective-permute-start.3
  33.8 3.1 collective-permute-start.2
  62.6 41.3 %gather_fusion.1 = bf16[20224,30]{1,0:T(8,128)(2,1)} fusion(bf16[30,31]{0,1:T(8,128)(2,1)S(1)} %copy.35, s32[20480]{0:T(1024)S(1)} %pad_clamp_fusion.1), kind=kCustom, calls=%fused_computation.1 | custom fusion | bytes 2507776 | tf_op jit(solution)/shard_map/gather | solution.py:69
  103.9 5.0 %copy.36 = bf16[20224,30]{0,1:T(8,128)(2,1)S(1)} copy(bf16[20224,30]{1,0:T(8,128)(2,1)} %gather_fusion.1) | data formatting | bytes 2426880 | tf_op jit(solution)/shard_map/gather | solution.py:69
  108.9 6.9 %reshape.890 = bf16[128,158,30]{1,0,2:T(8,128)(2,1)} reshape(bf16[20224,30]{0,1:T(8,128)(2,1)S(1)} %copy.36) | data formatting | bytes 2426880 | tf_op jit(solution)/shard_map/gather | solution.py:69
  115.8 41.0 %gather_fusion.2 = bf16[20224,12]{1,0:T(8,128)(2,1)} fusion(bf16[12,31]{0,1:T(8,128)(2,1)S(1)} %copy.37, s32[20480]{0:T(1024)S(1)} %pad_clamp_fusion), kind=kCustom, calls=%fused_computation.2 | custom fusion | bytes 1051648 | tf_op jit(solution)/shard_map/gather | solution.py:86
  156.8 4.2 copy.38
  163.7 1.0 gather_fusion.3
  164.8 1.9 gather_fusion.4
  166.6 2.4 fusion.8
  169.8 3.2 reshape.862
  173.2 3.2 reshape.865
  176.4 1.4 fusion.30
  177.8 1.9 gather_fusion.5
  179.6 2.5 fusion.14
  182.2 0.9 copy-done.1
  183.3 6.7 %reshape.868 = bf16[30,4,32,4,32]{4,3,2,1,0:T(4,128)(2,1)} reshape(bf16[30,128,128]{2,1,0:T(8,128)(2,1)} %copy-done.1) | data formatting | bytes 1966080 | tf_op jit(solution)/shard_map/reshape | solution.py:139
  190.0 2.2 fusion.31
  192.2 2.9 gather_fusion.6
  195.1 2.5 fusion.17
  197.6 1.0 copy-done
  198.6 1.1 pad.49
  199.7 6.3 %reshape.871 = bf16[30,4,32,4,32]{4,3,2,1,0:T(4,128)(2,1)} reshape(bf16[30,128,128]{2,1,0:T(8,128)(2,1)} %copy-done) | data formatting | bytes 1966080 | tf_op jit(solution)/shard_map/reshape | solution.py:139
  206.0 1.9 add_divide_fusion.3
  207.9 1.0 div.411
  209.6 1.7 mul.508
  211.3 1.0 div.417
  213.1 1.7 mul.517
  215.7 1.7 mul.514
  218.3 1.1 mul.511
  219.4 5.2 %copy.119 = bf16[30,4,32,4,32]{4,2,3,1,0:T(8,128)(2,1)} copy(bf16[30,4,32,4,32]{4,3,2,1,0:T(4,128)(2,1)} %reshape.862) | data formatting | bytes 1966080 | tf_op jit(solution)/shard_map/reshape | solution.py:139
  224.6 6.6 %reshape.863 = bf16[16,30,1024]{2,0,1:T(8,128)(2,1)} reshape(bf16[4,4,30,32,32]{4,3,1,0,2:T(8,128)(2,1)} %bitcast.342) | data formatting | bytes 1966080 | tf_op jit(solution)/shard_map/reshape | solution.py:141
  231.2 1.8 copy.41
  235.4 5.3 %copy.118 = bf16[30,4,32,4,32]{4,2,3,1,0:T(8,128)(2,1)} copy(bf16[30,4,32,4,32]{4,3,2,1,0:T(4,128)(2,1)} %reshape.865) | data formatting | bytes 1966080 | tf_op jit(solution)/shard_map/reshape | solution.py:139
  240.7 6.8 %reshape.866 = bf16[16,30,1024]{2,0,1:T(8,128)(2,1)} reshape(bf16[4,4,30,32,32]{4,3,1,0,2:T(8,128)(2,1)} %bitcast.343) | data formatting | bytes 1966080 | tf_op jit(solution)/shard_map/reshape | solution.py:141
  247.5 1.8 copy.46
  249.7 1.0 fusion.22
  251.9 0.9 fusion.100
  253.5 5.3 %copy.117 = bf16[30,4,32,4,32]{4,2,3,1,0:T(8,128)(2,1)} copy(bf16[30,4,32,4,32]{4,3,2,1,0:T(4,128)(2,1)} %reshape.868) | data formatting | bytes 1966080 | tf_op jit(solution)/shard_map/reshape | solution.py:139
  258.8 6.6 %reshape.869 = bf16[16,30,1024]{2,0,1:T(8,128)(2,1)} reshape(bf16[4,4,30,32,32]{4,3,1,0,2:T(8,128)(2,1)} %bitcast.344) | data formatting | bytes 1966080 | tf_op jit(solution)/shard_map/reshape | solution.py:141
  265.4 1.8 copy.51
  267.6 1.0 fusion.24
  269.8 0.9 fusion.98
  271.3 5.2 %copy.116 = bf16[30,4,32,4,32]{4,2,3,1,0:T(8,128)(2,1)} copy(bf16[30,4,32,4,32]{4,3,2,1,0:T(4,128)(2,1)} %reshape.871) | data formatting | bytes 1966080 | tf_op jit(solution)/shard_map/reshape | solution.py:139
  276.5 6.6 %reshape.872 = bf16[16,30,1024]{2,0,1:T(8,128)(2,1)} reshape(bf16[4,4,30,32,32]{4,3,1,0,2:T(8,128)(2,1)} %bitcast.345) | data formatting | bytes 1966080 | tf_op jit(solution)/shard_map/reshape | solution.py:141
  283.1 1.8 copy.56
  285.4 1.0 fusion.26
  291.4 0.9 fusion.96
  293.0 0.9 multiply_add_fusion
  294.7 1.1 fusion.75
  295.8 34.3 %custom-call.11 = f32[4,93,93]{2,1,0:T(8,128)S(1)} custom-call(f32[4,93,93]{2,1,0:T(8,128)S(1)} %fusion.75), custom_call_target="Cholesky" | custom-call | tf_op jit(solution)/shard_map/jit(cholesky)/cholesky | solution.py:59
  331.7 28.6 %custom-call.12 = f32[4,1,93,93]{2,3,1,0:T(8,128)S(1)} custom-call(f32[4,1,93,93]{3,2,1,0:T(8,128)S(1)} %select_bitcast_fusion), custom_call_target="InvertDiagBlocksLowerTriangular" | custom-call | tf_op jit(solution)/shard_map/jit(_cho_solve)/vmap()/triangular_solve | solution.py:60
  362.9 1.9 copy.87
  370.6 2.6 pad_maximum_fusion.6
  373.2 72.3 %psum.7 = f32[4]{0:T(128)S(1)} all-reduce(f32[4]{0:T(128)S(1)} %pad_maximum_fusion.6), channel_id=1, replica_groups=mesh['frow'=8,'fcol'=32] {'fcol'}, use_global_device_ids=true, to_apply=%region_23.24 | all-reduce | flops 4 | bytes 32 | tf_op jit(solution)/shard_map/psum | solution.py:188
  448.7 1.1 rsqrt_multiply_fusion.3
  449.8 1.1 rsqrt_multiply_fusion.1
  (213 shorter events, 49.8 us)
Async XLA Ops:
  0.9 30.7 %collective-permute-start.1 = (f32[2,128,128]{2,1,0:T(8,128)S(1)}, f32[2,128,128]{2,1,0:T(8,128)S(1)}, u32[]{:S(2)}, u32[]{:S(2)}) collective-permute-start(f32[2,128,128]{2,1,0:T(8,128)S(1)} %pad_maximum_fusion.3), channel_id=1, source_target_pairs={{32,0},{64,32},{96,64},{128,96},{160,128},{192,160},{224,192},{33,... | collective-permute-start | bytes 393224 | tf_op jit(solution)/shard_map/ppermute | solution.py:26
  4.5 27.2 %collective-permute-start = (f32[2,128,128]{2,1,0:T(8,128)S(1)}, f32[2,128,128]{2,1,0:T(8,128)S(1)}, u32[]{:S(2)}, u32[]{:S(2)}) collective-permute-start(f32[2,128,128]{2,1,0:T(8,128)S(1)} %pad_maximum_fusion.3), channel_id=1, source_target_pairs={{0,32},{32,64},{64,96},{96,128},{128,160},{160,192},{192,224},{1,3... | collective-permute-start | bytes 393224 | tf_op jit(solution)/shard_map/ppermute | solution.py:23
  14.7 146.6 %copy-start.29 = (f32[1,16]{1,0:T(1,128)}, f32[1,16]{1,0:T(1,128)S(1)}, u32[]{:S(2)}) copy-start(f32[1,16]{1,0:T(1,128)S(1)} %get-tuple-element.86) | copy-start | bytes 196
  14.7 146.6 %copy-start.31 = (f32[1,16]{1,0:T(1,128)}, f32[1,16]{1,0:T(1,128)S(1)}, u32[]{:S(2)}) copy-start(f32[1,16]{1,0:T(1,128)S(1)} %get-tuple-element.87) | copy-start | bytes 196
  16.5 146.8 %copy-start.23 = (pred[158,128]{1,0:T(8,128)(4,1)}, pred[158,128]{1,0:T(8,128)(4,1)S(1)}, u32[]{:S(2)}) copy-start(pred[158,128]{1,0:T(8,128)(4,1)S(1)} %fusion.90) | copy-start | bytes 60676
  29.6 131.7 %copy-start.33 = (f32[3]{0:T(128)}, f32[3]{0:T(128)S(1)}, u32[]{:S(2)}) copy-start(f32[3]{0:T(128)S(1)} %pad.36.clone) | copy-start | bytes 40
  31.6 129.6 %copy-start.35 = (f32[16]{0:T(128)}, f32[16]{0:T(128)S(1)}, u32[]{:S(2)}) copy-start(f32[16]{0:T(128)S(1)} %get-tuple-element.92) | copy-start | bytes 196
  31.6 129.6 %copy-start.36 = (f32[16]{0:T(128)}, f32[16]{0:T(128)S(1)}, u32[]{:S(2)}) copy-start(f32[16]{0:T(128)S(1)} %get-tuple-element.93) | copy-start | bytes 196
  32.5 129.4 %collective-permute-start.3 = (f32[2,384,128]{2,1,0:T(8,128)S(1)}, f32[2,384,128]{2,1,0:T(8,128)S(1)}, u32[]{:S(2)}, u32[]{:S(2)}) collective-permute-start(f32[2,384,128]{2,1,0:T(8,128)S(1)} %pad_maximum_fusion.1), channel_id=1, source_target_pairs={{1,0},{2,1},{3,2},{4,3},{5,4},{6,5},{7,6},{8,7},{9,8},{10,9},{11,1... | collective-permute-start | bytes 1179656 | tf_op jit(solution)/shard_map/ppermute | solution.py:26
  33.8 128.1 %collective-permute-start.2 = (f32[2,384,128]{2,1,0:T(8,128)S(1)}, f32[2,384,128]{2,1,0:T(8,128)S(1)}, u32[]{:S(2)}, u32[]{:S(2)}) collective-permute-start(f32[2,384,128]{2,1,0:T(8,128)S(1)} %pad_maximum_fusion.1), channel_id=1, source_target_pairs={{0,1},{1,2},{2,3},{3,4},{4,5},{5,6},{6,7},{7,8},{8,9},{9,10},{10,1... | collective-permute-start | bytes 1179656 | tf_op jit(solution)/shard_map/ppermute | solution.py:23
  156.8 5.2 %copy-start.5 = (f32[128,128]{1,0:T(8,128)S(1)}, f32[128,128]{1,0:T(8,128)}, u32[]{:S(2)}) copy-start(f32[128,128]{1,0:T(8,128)} %param.11) | copy-start | bytes 196612
  156.8 5.2 %copy-start.6 = (f32[128,128]{1,0:T(8,128)S(1)}, f32[128,128]{1,0:T(8,128)}, u32[]{:S(2)}) copy-start(f32[128,128]{1,0:T(8,128)} %param.10) | copy-start | bytes 196612
  161.0 2.4 copy-start.7
  161.2 0.9 copy-start.38
  161.2 0.9 copy-start.39
  163.7 2.9 copy-start.21
  166.6 2.4 copy-start.2
  166.6 2.5 copy-start.4
  173.2 3.2 copy-start.24
  176.4 3.3 copy-start.22
  182.2 1.0 copy-start.1
  197.6 1.0 copy-start
  199.7 6.3 %copy-start.8 = (s32[4,128,128]{2,1,0:T(8,128)S(1)}, s32[4,128,128]{2,1,0:T(8,128)}, u32[]{:S(2)}) copy-start(s32[4,128,128]{2,1,0:T(8,128)} %param.9) | copy-start | bytes 786436
  231.2 1.8 copy-start.15
  231.2 2.3 copy-start.12
  233.0 0.9 copy-start.19
  233.0 0.9 copy-start.28
  233.0 1.5 copy-start.30
  233.0 1.5 copy-start.32
  233.0 1.5 copy-start.34
  233.1 1.5 copy-start.37
  247.5 2.2 copy-start.11
  249.2 1.4 copy-start.27
  265.4 1.8 copy-start.14
  265.4 2.2 copy-start.10
  267.2 1.4 copy-start.26
  283.1 1.8 copy-start.13
  283.1 2.2 copy-start.9
  284.9 1.4 copy-start.25
  368.1 1.0 copy-start.3
  368.2 1.0 copy-start.18
  368.2 0.9 copy-start.20
  368.2 1.6 copy-start.16
  368.2 1.6 copy-start.17
where the time goes:
time: 457 us; the launch traced here: 452 us
  local copies, waits for them, and re-layouts  219 us (48%)
  other arithmetic  94.4 us (21%)
  blocking collectives  72.3 us (16%)
  between operations  32.4 us (7%)
  matrix products  24 us (5%)
  starting transfers between devices  10.2 us (2%)
    psum x1, blocking collectives, on_device(): strip_totals = lax.psum(jnp.stack(totals), 'fcol')  72.3 us
    gather x3, local copies, waits for them, and re-layouts, toeplitz_table(): table[:, clipped]  53.2 us
    gather x2, local copies, waits for them, and re-layouts, on_device(): table[:, jnp.clip(col_offsets, 0, 2 * R)]  45.2 us
    reshape x8, local copies, waits for them, and re-layouts, on_device(): blocks.reshape(NB, cells_down, STAMP, cells_across, STAMP)  40.4 us
    another operation x4, other arithmetic, solve_fit(): factor = jnp.linalg.cholesky(shifted)  35.8 us
    reshape x8, local copies, waits for them, and re-layouts, on_device(): basis_cells = blocks.reshape(NB, cells_down, STAMP, cells_across, STAMP)....  33.7 us
    another operation x3, other arithmetic, solve_fit(): jax.scipy.linalg.cho_solve((factor, True), normal_vector[..., None])[..., 0]  30 us
    unnamed x91, local copies, waits for them, and re-layouts  9.34 us
  transfers between devices with their start and end apart: 4, of which 0 were waited for; matrix products, arithmetic and copies ran while one was open for 27% of the time, Pallas kernels for 0%

commit v1 on v0

v1 whole, which is shorter than its diff:
```python
import functools

import jax
import jax.numpy as jnp
import numpy as np
from jax import lax
from jax.experimental import pallas as pl
from jax.experimental.pallas import tpu as pltpu
from jax.sharding import PartitionSpec as P

V = 4
TH = 128
TW = 128
R = 15
NB = 30
STAMP = 32
DMAX = 113
SMAX = 12
SPREADS = (0.75, 1.5, 3.0)
MARGIN = DMAX + R
F = 12
WROWS = 160
SLAB = 48
YB = 16
KDIM = F * SLAB + 2 * YB
PROWS = 392
BF = jnp.bfloat16
F32 = jnp.float32


def kernel_table():
    offsets = np.arange(-R, R + 1, dtype=np.float32)
    profiles = []
    for spread in SPREADS:
        for degree in range(4):
            profile = np.exp(-offsets * offsets / np.float32(2.0 * spread * spread)) * (
                offsets / np.float32(spread)
            ) ** degree
            profile = profile.astype(np.float32)
            profiles.append(profile / np.sqrt(np.sum(profile * profile)))
    return np.stack(profiles).astype(BF)


def basis_pairs():
    pairs = []
    for g in range(3):
        for a in range(4):
            for b in range(4 - a):
                pairs.append((4 * g + a, 4 * g + b))
    return pairs


def column_matrix(table):
    out = np.zeros((256, F * TW), BF)
    for f in range(F):
        for x in range(TW):
            out[x : x + 2 * R + 1, f * TW + x] = table[f]
    return out


def row_matrix(table):
    out = np.zeros((YB * 32, KDIM), BF)
    for k, (r, c) in enumerate(basis_pairs()):
        for y in range(YB):
            out[y * 32 + k, c * SLAB + y : c * SLAB + y + 2 * R + 1] = table[r]
    for y in range(YB):
        out[y * 32 + NB, F * SLAB + YB] = 1.0
        out[y * 32 + NB + 1, F * SLAB + y] = 1.0
    return out


def roll_lanes(x, shift):
    return pltpu.roll(x, shift, 1)


def body(dither, stamps, mid, left, right, science, mask, tcol, trow, diff_out, var_out, tot_out,
         planes, cbuf, sbuf, dbuf, gbuf, wbuf):
    for p in range(2):
        for b, ref in ((0, left), (1, mid), (2, right)):
            planes[p, b, 0:384, :] = ref[p]
            planes[p, b, 384:PROWS, :] = jnp.zeros((PROWS - 384, 128), F32)
    lane = lax.broadcasted_iota(jnp.int32, (8, 128), 1)
    sub = lax.broadcasted_iota(jnp.int32, (8, 128), 0)
    lane1 = lane[0:1]

    windows = []
    for v in range(V):
        dy = dither[v, 0]
        dx = dither[v, 1]
        row0 = DMAX + dy
        col0 = DMAX + dx
        b0 = lax.shift_right_logical(col0, 7)
        s = jnp.bitwise_and(col0, 127)
        back = jnp.bitwise_and(128 - s, 127)
        last = jnp.minimum(b0 + 2, 2)
        t0 = roll_lanes(planes[0, b0, pl.ds(row0, WROWS), :], back)
        t1 = roll_lanes(planes[0, b0 + 1, pl.ds(row0, WROWS), :], back)
        t2 = roll_lanes(planes[0, last, pl.ds(row0, WROWS), :], back)
        keep = lane1 < 128 - s
        windows.append(
            jnp.concatenate([jnp.where(keep, t0, t1), jnp.where(keep, t1, t2)], axis=1).astype(BF)
        )
        col1 = MARGIN + dx
        b1 = lax.shift_right_logical(col1, 7)
        s1 = jnp.bitwise_and(col1, 127)
        back1 = jnp.bitwise_and(128 - s1, 127)
        nxt = jnp.minimum(b1 + 1, 2)
        q0 = roll_lanes(planes[1, b1, pl.ds(MARGIN + dy, TH), :], back1)
        q1 = roll_lanes(planes[1, nxt, pl.ds(MARGIN + dy, TH), :], back1)
        var = jnp.where(lane1 < 128 - s1, q0, q1)
        var_out[v] = var
        usable = (mask[v] == 0).astype(F32)
        wbuf[v] = usable / (0.25 + var)
        sbuf[:, v * TW : (v + 1) * TW] = science[v].astype(BF)

    for v in range(V):
        cp = jnp.dot(windows[v], tcol[...], preferred_element_type=F32).astype(BF)
        for f in range(F):
            cbuf[f, :, v * TW : (v + 1) * TW] = cp[:, f * TW : (f + 1) * TW]

    ones_piece = jnp.ones((YB, V * TW), BF)

    def row_block(yb, carry):
        base = pl.multiple_of(yb * YB, YB)
        slab = jnp.concatenate(
            [cbuf[f, pl.ds(base, SLAB), :] for f in range(F)]
            + [sbuf[pl.ds(base, YB), :], ones_piece],
            axis=0,
        )
        out = jnp.dot(trow[...], slab, preferred_element_type=F32).astype(BF)
        dbuf[pl.ds(pl.multiple_of(yb * (YB * 32), YB * 32), YB * 32), :] = out
        return carry

    lax.fori_loop(0, TH // YB, row_block, 0)

    group_masks = [
        ((lax.broadcasted_iota(jnp.int32, (32, 128), 1) // 32) == j).astype(F32).astype(BF)
        for j in range(4)
    ]
    for v in range(V):

        def gram_row(i, carry, v=v):
            acc = jnp.zeros((32, 128), F32)
            for c in range(8):
                ws = []
                ds = [[] for _ in range(4)]
                for t in range(4):
                    y = i * 32 + c * 4 + t
                    d = dbuf[pl.ds(pl.multiple_of(y * 32, 32), 32), v * TW : (v + 1) * TW]
                    w = wbuf[v, pl.ds(y, 1), :]
                    ws.append((d.astype(F32) * w).astype(BF))
                    for j in range(4):
                        ds[j].append(d * group_masks[j])
                wcat = jnp.concatenate(ws, axis=1)
                dcat = jnp.concatenate([jnp.concatenate(q, axis=1) for q in ds], axis=0)
                acc = acc + lax.dot_general(
                    wcat, dcat, (((1,), (1,)), ((), ())), preferred_element_type=F32
                )
            gbuf[v, i] = acc
            return carry

        lax.fori_loop(0, 4, gram_row, 0)

    group = lane // 32
    xs = (group.astype(F32) - 1.5) * 0.5
    mats = []
    for v in range(V):
        use = jnp.zeros((8, 128), F32)
        cell = sub * 4 + group
        for s in range(SMAX):
            use = use + (cell == stamps[v, s]).astype(F32)
        m00 = jnp.zeros((32, 128), F32)
        m02 = jnp.zeros((32, 128), F32)
        m22 = jnp.zeros((32, 128), F32)
        for i in range(4):
            h = gbuf[v, i] * use[i : i + 1, :]
            ys = (i - 1.5) * 0.5
            m00 = m00 + h
            m02 = m02 + h * ys
            m22 = m22 + h * (ys * ys)
        x1 = xs[0:1]

        def fold(m):
            m = m + roll_lanes(m, 32)
            return m + roll_lanes(m, 64)

        m01 = fold(m00 * x1)
        m11 = fold(m00 * (x1 * x1))
        m12 = fold(m02 * x1)
        m00 = fold(m00)
        m02 = fold(m02)
        m22 = fold(m22)
        g1 = lane1 // 32
        zero = jnp.zeros((32, 128), F32)

        def block_row(a, b, c):
            return jnp.where(g1 == 0, a, jnp.where(g1 == 1, b, jnp.where(g1 == 2, c, zero)))

        mat = jnp.concatenate(
            [
                block_row(m00, m01, m02),
                block_row(m01, m11, m12),
                block_row(m02, m12, m22),
                zero,
            ],
            axis=0,
        )
        rows = lax.broadcasted_iota(jnp.int32, (128, 128), 0)
        cols = lax.broadcasted_iota(jnp.int32, (128, 128), 1)
        valid_col = (cols % 32) != 31
        mat = jnp.where(valid_col & ((rows % 32) != 31), 0.5 * (mat + mat.T), mat)
        diag = (rows == cols) & valid_col & (rows < 96)
        trace = jnp.sum(jnp.where(diag, mat, 0.0), keepdims=True)
        mat = jnp.where(diag, mat + 0.001 * trace / 93.0, mat)
        mats.append([mat[8 * r : 8 * r + 8] for r in range(12)])

    for r in range(12):
        pivots = [i for i in range(8) if (8 * r + i) % 32 != 31]
        panel = [mats[v][r] for v in range(V)]
        for i in pivots:
            p = 8 * r + i
            for v in range(V):
                cur = panel[v]
                colb = jnp.broadcast_to(cur[:, p : p + 1], (8, 128))
                rs = cur[i : i + 1, :] / colb[i : i + 1, :]
                panel[v] = jnp.where(sub == i, rs, cur - colb * rs)
        for v in range(V):
            for b in range(12):
                if b == r:
                    continue
                src = mats[v][b]
                acc = src
                for i in pivots:
                    p = 8 * r + i
                    colb = jnp.broadcast_to(src[:, p : p + 1], (8, 128))
                    acc = acc - colb * panel[v][i : i + 1, :]
                mats[v][b] = acc
            mats[v][r] = panel[v]

    row_coord = (lax.broadcasted_iota(jnp.int32, (8, 128), 0).astype(F32) + 0.5 - 64.0) / 64.0
    col_coord = (lane.astype(F32) + 0.5 - 64.0) / 64.0
    tot_rows = []
    for v in range(V):
        vec = jnp.zeros((8, 128), F32)
        for b in range(12):
            colb = jnp.broadcast_to(mats[v][b][:, 31:32], (8, 128))
            vec = vec + jnp.where(lane == sub + 8 * b, colb, 0.0)
        vec = jnp.sum(vec, axis=0, keepdims=True)
        highs = []
        lows = []
        for a in range(3):
            ca = jnp.broadcast_to(jnp.where(lane1 // 32 == a, vec, 0.0), (8, 128))
            ca = ca + roll_lanes(ca, 32)
            ca = ca + roll_lanes(ca, 64)
            ca = jnp.where(lane % 32 == 31, 0.0, ca)
            high = ca.astype(BF).astype(F32)
            low = ca - high
            for dst, val in ((highs, high), (lows, low)):
                dst.append(
                    jnp.concatenate(
                        [jnp.where(sub == lane // 32 + 4 * h, val, 0.0) for h in range(2)], axis=1
                    )
                )
        lhs = jnp.concatenate(highs + lows, axis=0).astype(BF)
        total = jnp.zeros((8, 128), F32)
        for yb in range(TH // 8):
            block = dbuf[yb * 256 : (yb + 1) * 256, v * TW : (v + 1) * TW]
            o = jnp.dot(lhs, block, preferred_element_type=F32)
            o = o[:24] + o[24:]
            model = o[0:8] + col_coord * o[8:16] + (row_coord + yb / 8.0) * o[16:24]
            rows8 = pl.ds(yb * 8, 8)
            diff = science[v, rows8, :] - model
            diff_out[v, rows8, :] = diff
            total = total + jnp.where(mask[v, rows8, :] == 0, diff * diff, 0.0)
        tot_rows.append(jnp.sum(total, axis=0, keepdims=True))
    tot_rows += [jnp.zeros((1, 128), F32)] * 4
    tot_out[...] = jnp.broadcast_to(
        jnp.sum(jnp.concatenate(tot_rows, axis=0), axis=1, keepdims=True), (8, 128)
    )


def fit_kernel(dither, stamps, mid, left, right, science, mask):
    table = kernel_table()
    vmem = pl.BlockSpec(memory_space=pltpu.VMEM)
    smem = pl.BlockSpec(memory_space=pltpu.SMEM)
    return pl.pallas_call(
        body,
        out_shape=(
            jax.ShapeDtypeStruct((V, TH, TW), F32),
            jax.ShapeDtypeStruct((V, TH, TW), F32),
            jax.ShapeDtypeStruct((8, 128), F32),
        ),
        in_specs=[smem, smem] + [vmem] * 7,
        out_specs=(vmem, vmem, vmem),
        scratch_shapes=[
            pltpu.VMEM((2, 3, PROWS, 128), F32),
            pltpu.VMEM((F, WROWS, V * TW), BF),
            pltpu.VMEM((TH, V * TW), BF),
            pltpu.VMEM((TH * 32, V * TW), BF),
            pltpu.VMEM((V, 4, 32, 128), F32),
            pltpu.VMEM((V, TH, TW), F32),
        ],
        compiler_params=pltpu.CompilerParams(vmem_limit_bytes=56 * 1024 * 1024),
        name="fit",
    )(dither, stamps, mid, left, right, science, mask,
      jnp.asarray(column_matrix(table)), jnp.asarray(row_matrix(table)))


def shift(x, axis, step):
    count = lax.axis_size(axis)
    return lax.ppermute(
        x, axis, [(i, i + step) for i in range(count) if 0 <= i + step < count]
    )


def strip_sum(x):
    for k in (1, 2, 4, 8, 16):
        x = x + lax.ppermute(x, "fcol", [(i, i ^ k) for i in range(lax.axis_size("fcol"))])
    return x


def on_device(science, pixel_mask, coadd_image, coadd_variance, dither, stamps):
    planes = jnp.stack([coadd_image, coadd_variance])
    above = shift(planes, "frow", 1)
    below = shift(planes, "frow", -1)
    mid = jnp.concatenate([above, planes, below], axis=1)
    left = shift(mid, "fcol", 1)
    right = shift(mid, "fcol", -1)
    diff, var, tot = fit_kernel(
        dither, stamps.reshape(V, SMAX), mid, left, right, science, pixel_mask
    )
    tot = strip_sum(tot)
    pixel_count = TH * TW * lax.axis_size("fcol")
    noise = tot[:V, :1].reshape(V, 1, 1) / pixel_count
    return diff * lax.rsqrt(noise + var + 1e-06)


def solution(mesh):
    in_specs = (
        P(None, "frow", "fcol"),
        P(None, "frow", "fcol"),
        P("frow", "fcol"),
        P("frow", "fcol"),
        P(),
        P(None, "frow", "fcol", None),
    )
    out_specs = P(None, "frow", "fcol")
    return jax.shard_map(
        on_device, mesh=mesh, in_specs=in_specs, out_specs=out_specs, check_vma=False
    )
```

time: 457 us -> 85.3 us (0.19); the launches traced: 452 us -> 85 us
  local copies, waits for them, and re-layouts: 219 us -> 1.43 us
  other arithmetic: 94.4 us -> 3.61 us
  blocking collectives: 72.3 us -> 0 us
  between operations: 32.4 us -> 0.08 us
  Pallas kernels: 0 us -> 30.9 us
  starting transfers between devices: 10.2 us -> 35.4 us
  matrix products: 24 us -> 0 us
  waiting for transfers between devices: 0.01 us -> 13.5 us
    gather x11 -> x0, local copies, waits for them, and re-layouts: 107 us -> none  [the longest x3 53.2 us: toeplitz_table(): table[:, clipped]]
    reshape x16 -> x0, local copies, waits for them, and re-layouts: 74.1 us -> none  [the longest x8 40.4 us: on_device(): blocks.reshape(NB, cells_down, STAMP, cells_across, STAMP)]
    psum x1 -> x0, blocking collectives: 72.3 us -> none  [on_device(): strip_totals = lax.psum(jnp.stack(totals), 'fcol')]
    another operation x16 -> x0, other arithmetic: 69.9 us -> none  [the longest x4 35.8 us: solve_fit(): factor = jnp.linalg.cholesky(shifted)]
    pallas_call x0 -> x1, Pallas kernels: none -> 30.9 us  [fit_kernel(): pl.pallas_call(body, out_shape=(jax.ShapeDtypeStruct((V, TH, TW), F32), j...]
    ppermute x4 -> x9, starting transfers between devices: 10.2 us -> 35.4 us  [the longest x5 25.2 us: strip_sum(): lax.ppermute(x, 'fcol', [(i, i ^ k) for i in range(lax.axis_size('fcol'))])]
    dot_general x28 -> x0, matrix products: 23.3 us -> none  [the longest x4 8.09 us: on_device(): jnp.einsum('kyj,kjx->kyx', row_toeplitz, chosen, preferred_element_type=j...]
    ppermute x4 -> x9, waiting for transfers between devices: 0.01 us -> 13.5 us  [the longest x5 7.37 us: strip_sum(): lax.ppermute(x, 'fcol', [(i, i ^ k) for i in range(lax.axis_size('fcol'))])]
  transfers between devices with their start and end apart: 4 -> 9, of which waited for: 0 -> 8; matrix products, arithmetic and copies ran while one was open for 27% -> 1% of each run, Pallas kernels for 0% -> 0%
where the time goes in v1:
time: 85.3 us; the launch traced here: 85 us
  starting transfers between devices  35.4 us (42%)
  Pallas kernels  30.9 us (36%)
  waiting for transfers between devices  13.5 us (16%)
  other arithmetic  3.61 us (4%)
  local copies, waits for them, and re-layouts  1.43 us (2%)
    pallas_call x1, Pallas kernels, fit_kernel(): pl.pallas_call(body, out_shape=(jax.ShapeDtypeStruct((V, TH, TW), F32), j...  30.9 us
    ppermute x5, starting transfers between devices, strip_sum(): lax.ppermute(x, 'fcol', [(i, i ^ k) for i in range(lax.axis_size('fcol'))])  25.2 us
    ppermute x4, starting transfers between devices, shift(): lax.ppermute(x, axis, [(i, i + step) for i in range(count) if 0 <= i + st...  10.2 us
    ppermute x5, waiting for transfers between devices, strip_sum(): lax.ppermute(x, 'fcol', [(i, i ^ k) for i in range(lax.axis_size('fcol'))])  7.37 us
    ppermute x4, waiting for transfers between devices, shift(): lax.ppermute(x, axis, [(i, i + step) for i in range(count) if 0 <= i + st...  6.11 us
    mul x1, other arithmetic, on_device(): return diff * lax.rsqrt(noise + var + 1e-06)  1.84 us
  transfers between devices with their start and end apart: 9, of which 8 were waited for; matrix products, arithmetic and copies ran while one was open for 1% of the time, Pallas kernels for 0%

profile of v1, /device:TPU:24, one launch (start us, length us, event | category | flops | bytes accessed | tf_op | source)
XLA Modules:
  0.0 85.0 jit_solution(13074097552830127931)
XLA Ops:
  0.0 0.0 copy-start.3
  0.0 0.0 copy-start.4
  0.0 0.9 %pad_maximum_fusion.1 = f32[2,128,128]{2,1,0:T(8,128)S(1)} fusion(f32[1,128,128]{2,1,0:T(8,128)} %bitcast.3, f32[1,128,128]{2,1,0:T(8,128)} %bitcast.5), kind=kLoop, calls=%fused_computation.2 | loop fusion | flops 32768 | bytes 262144 | tf_op jit(solution)/shard_map/stack | solution.py:323
  0.9 0.0 copy-start.5
  0.9 3.6 %collective-permute-start.1 = (f32[2,128,128]{2,1,0:T(8,128)S(1)}, f32[2,128,128]{2,1,0:T(8,128)S(1)}, u32[]{:S(2)}, u32[]{:S(2)}) collective-permute-start(f32[2,128,128]{2,1,0:T(8,128)S(1)} %pad_maximum_fusion.1), channel_id=1, source_target_pairs={{32,0},{64,32},{96,64},{128,96},{160,128},{192,160},{224,192},{33,... | collective-permute-start | bytes 393224 | tf_op jit(solution)/shard_map/ppermute | solution.py:311
  4.5 2.3 %collective-permute-start = (f32[2,128,128]{2,1,0:T(8,128)S(1)}, f32[2,128,128]{2,1,0:T(8,128)S(1)}, u32[]{:S(2)}, u32[]{:S(2)}) collective-permute-start(f32[2,128,128]{2,1,0:T(8,128)S(1)} %pad_maximum_fusion.1), channel_id=1, source_target_pairs={{0,32},{32,64},{64,96},{96,128},{128,160},{160,192},{192,224},{1,3... | collective-permute-start | bytes 393224 | tf_op jit(solution)/shard_map/ppermute | solution.py:311
  6.8 1.3 %collective-permute-done.1 = f32[2,128,128]{2,1,0:T(8,128)S(1)} collective-permute-done((f32[2,128,128]{2,1,0:T(8,128)S(1)}, f32[2,128,128]{2,1,0:T(8,128)S(1)}, u32[]{:S(2)}, u32[]{:S(2)}) %collective-permute-start.1) | collective-permute-done | bytes 131104 | tf_op jit(solution)/shard_map/ppermute | solution.py:311
  8.1 4.2 %collective-permute-done = f32[2,128,128]{2,1,0:T(8,128)S(1)} collective-permute-done((f32[2,128,128]{2,1,0:T(8,128)S(1)}, f32[2,128,128]{2,1,0:T(8,128)S(1)}, u32[]{:S(2)}, u32[]{:S(2)}) %collective-permute-start) | collective-permute-done | bytes 131104 | tf_op jit(solution)/shard_map/ppermute | solution.py:311
  12.3 0.0 copy-done.3
  12.3 0.0 copy-done.4
  12.3 0.0 copy-start
  12.3 1.3 %collective-permute-start.3 = (f32[2,384,128]{2,1,0:T(8,128)S(1)}, f32[2,384,128]{2,1,0:T(8,128)S(1)}, u32[]{:S(2)}, u32[]{:S(2)}) collective-permute-start(f32[2,384,128]{2,1,0:T(8,128)S(1)} %pad_maximum_fusion.mid), channel_id=1, source_target_pairs={{1,0},{2,1},{3,2},{4,3},{5,4},{6,5},{7,6},{8,7},{9,8},{10,9},{11,1... | collective-permute-start | bytes 1179656 | tf_op jit(solution)/shard_map/ppermute | solution.py:311
  13.6 3.1 %collective-permute-start.2 = (f32[2,384,128]{2,1,0:T(8,128)S(1)}, f32[2,384,128]{2,1,0:T(8,128)S(1)}, u32[]{:S(2)}, u32[]{:S(2)}) collective-permute-start(f32[2,384,128]{2,1,0:T(8,128)S(1)} %pad_maximum_fusion.mid), channel_id=1, source_target_pairs={{0,1},{1,2},{2,3},{3,4},{4,5},{5,6},{6,7},{7,8},{8,9},{9,10},{10,1... | collective-permute-start | bytes 1179656 | tf_op jit(solution)/shard_map/ppermute | solution.py:311
  16.7 0.0 copy-done.5
  16.7 0.7 copy.10.dither
  17.4 0.0 collective-permute-done.3.right
  17.4 0.0 copy-start.1
  17.4 0.6 collective-permute-done.2.left
  18.0 0.0 copy-start.2
  18.0 0.0 copy-done
  18.0 0.1 copy-done.1
  18.1 0.6 copy-done.2
  18.8 30.9 %fit.1 = (f32[4,128,128]{2,1,0:T(8,128)}, f32[4,128,128]{2,1,0:T(8,128)}, f32[8,128]{1,0:T(8,128)}) custom-call(s32[4,2]{1,0:T(4,128)} %copy.10.dither, s32[4,12]{1,0:T(4,128)} %bitcast.7, f32[2,384,128]{2,1,0:T(8,128)} %copy-done, f32[2,384,128]{2,1,0:T(8,128)} %copy-done.2, f32[2,384,128]{2,1,0:T(8,128)} %copy-done.1, f32[4,128,128]{2,1,0:T(8,128)} %science.1, ...), custom_call_target="tpu_custom_call" | custom-call | tf_op jit(solution)/shard_map/fit/pallas_call | solution.py:286
  49.7 7.5 %collective-permute-start.4 = (f32[8,128]{1,0:T(8,128)}, f32[8,128]{1,0:T(8,128)S(1)}, u32[]{:S(2)}, u32[]{:S(2)}) collective-permute-start(f32[8,128]{1,0:T(8,128)} %get-tuple-element.9), channel_id=1, source_target_pairs={{0,1},{1,0},{2,3},{3,2},{4,5},{5,4},{6,7},{7,6},{8,9},{9,8},{10,11... | collective-permute-start | bytes 12296 | tf_op jit(solution)/shard_map/ppermute | solution.py:318
  57.2 1.0 %collective-permute-done.4 = f32[8,128]{1,0:T(8,128)S(1)} collective-permute-done((f32[8,128]{1,0:T(8,128)}, f32[8,128]{1,0:T(8,128)S(1)}, u32[]{:S(2)}, u32[]{:S(2)}) %collective-permute-start.4) | collective-permute-done | bytes 4128 | tf_op jit(solution)/shard_map/ppermute | solution.py:318
  58.2 0.7 add.29
  58.9 4.2 %collective-permute-start.5 = (f32[8,128]{1,0:T(8,128)S(1)}, f32[8,128]{1,0:T(8,128)S(1)}, u32[]{:S(2)}, u32[]{:S(2)}) collective-permute-start(f32[8,128]{1,0:T(8,128)S(1)} %add.29), channel_id=1, source_target_pairs={{0,2},{1,3},{2,0},{3,1},{4,6},{5,7},{6,4},{7,5},{8,10},{9,11},{10,... | collective-permute-start | bytes 12296 | tf_op jit(solution)/shard_map/ppermute | solution.py:318
  63.1 1.6 %collective-permute-done.5 = f32[8,128]{1,0:T(8,128)S(1)} collective-permute-done((f32[8,128]{1,0:T(8,128)S(1)}, f32[8,128]{1,0:T(8,128)S(1)}, u32[]{:S(2)}, u32[]{:S(2)}) %collective-permute-start.5) | collective-permute-done | bytes 4128 | tf_op jit(solution)/shard_map/ppermute | solution.py:318
  64.7 2.7 %collective-permute-start.6 = (f32[8,128]{1,0:T(8,128)S(1)}, f32[8,128]{1,0:T(8,128)S(1)}, u32[]{:S(2)}, u32[]{:S(2)}) collective-permute-start(f32[8,128]{1,0:T(8,128)S(1)} %add.30), channel_id=1, source_target_pairs={{0,4},{1,5},{2,6},{3,7},{4,0},{5,1},{6,2},{7,3},{8,12},{9,13},{10,... | collective-permute-start | bytes 12296 | tf_op jit(solution)/shard_map/ppermute | solution.py:318
  67.3 1.6 %collective-permute-done.6 = f32[8,128]{1,0:T(8,128)S(1)} collective-permute-done((f32[8,128]{1,0:T(8,128)S(1)}, f32[8,128]{1,0:T(8,128)S(1)}, u32[]{:S(2)}, u32[]{:S(2)}) %collective-permute-start.6) | collective-permute-done | bytes 4128 | tf_op jit(solution)/shard_map/ppermute | solution.py:318
  68.9 3.8 %collective-permute-start.7 = (f32[8,128]{1,0:T(8,128)S(1)}, f32[8,128]{1,0:T(8,128)S(1)}, u32[]{:S(2)}, u32[]{:S(2)}) collective-permute-start(f32[8,128]{1,0:T(8,128)S(1)} %add.31), channel_id=1, source_target_pairs={{0,8},{1,9},{2,10},{3,11},{4,12},{5,13},{6,14},{7,15},{8,0},{9,1},... | collective-permute-start | bytes 12296 | tf_op jit(solution)/shard_map/ppermute | solution.py:318
  72.7 1.6 %collective-permute-done.7 = f32[8,128]{1,0:T(8,128)S(1)} collective-permute-done((f32[8,128]{1,0:T(8,128)S(1)}, f32[8,128]{1,0:T(8,128)S(1)}, u32[]{:S(2)}, u32[]{:S(2)}) %collective-permute-start.7) | collective-permute-done | bytes 4128 | tf_op jit(solution)/shard_map/ppermute | solution.py:318
  74.3 7.1 %collective-permute-start.8 = (f32[8,128]{1,0:T(8,128)S(1)}, f32[8,128]{1,0:T(8,128)S(1)}, u32[]{:S(2)}, u32[]{:S(2)}) collective-permute-start(f32[8,128]{1,0:T(8,128)S(1)} %add.32), channel_id=1, source_target_pairs={{0,16},{1,17},{2,18},{3,19},{4,20},{5,21},{6,22},{7,23},{8,24},{9,... | collective-permute-start | bytes 12296 | tf_op jit(solution)/shard_map/ppermute | solution.py:318
  81.4 1.6 %collective-permute-done.8 = f32[8,128]{1,0:T(8,128)S(1)} collective-permute-done((f32[8,128]{1,0:T(8,128)S(1)}, f32[8,128]{1,0:T(8,128)S(1)}, u32[]{:S(2)}, u32[]{:S(2)}) %collective-permute-start.8) | collective-permute-done | bytes 4128 | tf_op jit(solution)/shard_map/ppermute | solution.py:318
  83.0 0.1 multiply_reduce_fusion
  83.1 1.8 %rsqrt_multiply_fusion = f32[4,128,128]{2,1,0:T(8,128)} fusion(f32[4,128,128]{2,1,0:T(8,128)} %get-tuple-element.8, f32[4,128,128]{2,1,0:T(8,128)} %get-tuple-element.10, f32[4]{0:T(128)S(1)} %multiply_reduce_fusion), kind=kLoop, calls=%fused_computation.1 | loop fusion | flops 196608 | bytes 786448 | tf_op jit(solution)/shard_map/mul | solution.py:335
  (5 shorter events, 0.0 us)
Async XLA Ops:
  0.0 12.3 %copy-start.3 = (f32[128,128]{1,0:T(8,128)S(1)}, f32[128,128]{1,0:T(8,128)}, u32[]{:S(2)}) copy-start(f32[128,128]{1,0:T(8,128)} %param.11) | copy-start | bytes 196612
  0.0 12.3 %copy-start.4 = (f32[128,128]{1,0:T(8,128)S(1)}, f32[128,128]{1,0:T(8,128)}, u32[]{:S(2)}) copy-start(f32[128,128]{1,0:T(8,128)} %param.10) | copy-start | bytes 196612
  0.9 15.8 %copy-start.5 = (s32[4,2]{0,1:T(2,128)S(1)}, s32[4,2]{0,1:T(2,128)}, u32[]{:S(2)}) copy-start(s32[4,2]{0,1:T(2,128)} %param.12) | copy-start | bytes 100
  0.9 7.1 %collective-permute-start.1 = (f32[2,128,128]{2,1,0:T(8,128)S(1)}, f32[2,128,128]{2,1,0:T(8,128)S(1)}, u32[]{:S(2)}, u32[]{:S(2)}) collective-permute-start(f32[2,128,128]{2,1,0:T(8,128)S(1)} %pad_maximum_fusion.1), channel_id=1, source_target_pairs={{32,0},{64,32},{96,64},{128,96},{160,128},{192,160},{224,192},{33,... | collective-permute-start | bytes 393224 | tf_op jit(solution)/shard_map/ppermute | solution.py:311
  4.5 7.8 %collective-permute-start = (f32[2,128,128]{2,1,0:T(8,128)S(1)}, f32[2,128,128]{2,1,0:T(8,128)S(1)}, u32[]{:S(2)}, u32[]{:S(2)}) collective-permute-start(f32[2,128,128]{2,1,0:T(8,128)S(1)} %pad_maximum_fusion.1), channel_id=1, source_target_pairs={{0,32},{32,64},{64,96},{96,128},{128,160},{160,192},{192,224},{1,3... | collective-permute-start | bytes 393224 | tf_op jit(solution)/shard_map/ppermute | solution.py:311
  12.3 5.7 %copy-start = (f32[2,384,128]{2,1,0:T(8,128)}, f32[2,384,128]{2,1,0:T(8,128)S(1)}, u32[]{:S(2)}) copy-start(f32[2,384,128]{2,1,0:T(8,128)S(1)} %pad_maximum_fusion.mid) | copy-start | bytes 1179652
  12.3 5.0 %collective-permute-start.3 = (f32[2,384,128]{2,1,0:T(8,128)S(1)}, f32[2,384,128]{2,1,0:T(8,128)S(1)}, u32[]{:S(2)}, u32[]{:S(2)}) collective-permute-start(f32[2,384,128]{2,1,0:T(8,128)S(1)} %pad_maximum_fusion.mid), channel_id=1, source_target_pairs={{1,0},{2,1},{3,2},{4,3},{5,4},{6,5},{7,6},{8,7},{9,8},{10,9},{11,1... | collective-permute-start | bytes 1179656 | tf_op jit(solution)/shard_map/ppermute | solution.py:311
  13.6 4.4 %collective-permute-start.2 = (f32[2,384,128]{2,1,0:T(8,128)S(1)}, f32[2,384,128]{2,1,0:T(8,128)S(1)}, u32[]{:S(2)}, u32[]{:S(2)}) collective-permute-start(f32[2,384,128]{2,1,0:T(8,128)S(1)} %pad_maximum_fusion.mid), channel_id=1, source_target_pairs={{0,1},{1,2},{2,3},{3,4},{4,5},{5,6},{6,7},{7,8},{8,9},{9,10},{10,1... | collective-permute-start | bytes 1179656 | tf_op jit(solution)/shard_map/ppermute | solution.py:311
  17.4 0.7 copy-start.1
  18.0 0.7 copy-start.2
  49.7 8.5 %collective-permute-start.4 = (f32[8,128]{1,0:T(8,128)}, f32[8,128]{1,0:T(8,128)S(1)}, u32[]{:S(2)}, u32[]{:S(2)}) collective-permute-start(f32[8,128]{1,0:T(8,128)} %get-tuple-element.9), channel_id=1, source_target_pairs={{0,1},{1,0},{2,3},{3,2},{4,5},{5,4},{6,7},{7,6},{8,9},{9,8},{10,11... | collective-permute-start | bytes 12296 | tf_op jit(solution)/shard_map/ppermute | solution.py:318
  58.9 5.8 %collective-permute-start.5 = (f32[8,128]{1,0:T(8,128)S(1)}, f32[8,128]{1,0:T(8,128)S(1)}, u32[]{:S(2)}, u32[]{:S(2)}) collective-permute-start(f32[8,128]{1,0:T(8,128)S(1)} %add.29), channel_id=1, source_target_pairs={{0,2},{1,3},{2,0},{3,1},{4,6},{5,7},{6,4},{7,5},{8,10},{9,11},{10,... | collective-permute-start | bytes 12296 | tf_op jit(solution)/shard_map/ppermute | solution.py:318
  64.7 4.2 %collective-permute-start.6 = (f32[8,128]{1,0:T(8,128)S(1)}, f32[8,128]{1,0:T(8,128)S(1)}, u32[]{:S(2)}, u32[]{:S(2)}) collective-permute-start(f32[8,128]{1,0:T(8,128)S(1)} %add.30), channel_id=1, source_target_pairs={{0,4},{1,5},{2,6},{3,7},{4,0},{5,1},{6,2},{7,3},{8,12},{9,13},{10,... | collective-permute-start | bytes 12296 | tf_op jit(solution)/shard_map/ppermute | solution.py:318
  68.9 5.3 %collective-permute-start.7 = (f32[8,128]{1,0:T(8,128)S(1)}, f32[8,128]{1,0:T(8,128)S(1)}, u32[]{:S(2)}, u32[]{:S(2)}) collective-permute-start(f32[8,128]{1,0:T(8,128)S(1)} %add.31), channel_id=1, source_target_pairs={{0,8},{1,9},{2,10},{3,11},{4,12},{5,13},{6,14},{7,15},{8,0},{9,1},... | collective-permute-start | bytes 12296 | tf_op jit(solution)/shard_map/ppermute | solution.py:318
  74.3 8.7 %collective-permute-start.8 = (f32[8,128]{1,0:T(8,128)S(1)}, f32[8,128]{1,0:T(8,128)S(1)}, u32[]{:S(2)}, u32[]{:S(2)}) collective-permute-start(f32[8,128]{1,0:T(8,128)S(1)} %add.32), channel_id=1, source_target_pairs={{0,16},{1,17},{2,18},{3,19},{4,20},{5,21},{6,22},{7,23},{8,24},{9,... | collective-permute-start | bytes 12296 | tf_op jit(solution)/shard_map/ppermute | solution.py:318

commit v2 on v1

--- a/solution.py
+++ b/solution.py
@@ -214,28 +214,55 @@
         mat = jnp.where(diag, mat + 0.001 * trace / 93.0, mat)
         mats.append([mat[8 * r : 8 * r + 8] for r in range(12)])
 
-    for r in range(12):
-        pivots = [i for i in range(8) if (8 * r + i) % 32 != 31]
-        panel = [mats[v][r] for v in range(V)]
-        for i in pivots:
-            p = 8 * r + i
+    def lane_of(x, p):
+        return jnp.broadcast_to(x[:, p : p + 1], (8, 128))
+
+    for a in range(3):
+        block = [[mats[v][4 * a + q] for q in range(4)] for v in range(V)]
+        for q in range(4):
+            pivots = [i for i in range(8) if 8 * q + i != 31]
+            lanes = {i: 32 * a + 8 * q + i for i in pivots}
+            cols = [{} for _ in range(V)]
+            others = [{} for _ in range(V)]
+            for i in pivots:
+                for v in range(V):
+                    cols[v][i] = lane_of(block[v][q], lanes[i])
+            for i in pivots:
+                for o in range(4):
+                    if o != q:
+                        for v in range(V):
+                            others[v][o, i] = lane_of(block[v][o], lanes[i])
+            for i in pivots:
+                for v in range(V):
+                    col = cols[v][i]
+                    inv = 1.0 / col[i : i + 1]
+                    mult = jnp.where(sub == i, -1.0, col)
+
+                    def step(x):
+                        return jnp.where(sub == i, 0.0, x) - mult * (x[i : i + 1] * inv)
+
+                    block[v][q] = step(block[v][q])
+                    for j in pivots:
+                        if j > i:
+                            cols[v][j] = step(cols[v][j])
             for v in range(V):
-                cur = panel[v]
-                colb = jnp.broadcast_to(cur[:, p : p + 1], (8, 128))
-                rs = cur[i : i + 1, :] / colb[i : i + 1, :]
-                panel[v] = jnp.where(sub == i, rs, cur - colb * rs)
+                for o in range(4):
+                    if o != q:
+                        acc = block[v][o]
+                        for i in pivots:
+                            acc = acc - others[v][o, i] * block[v][q][i : i + 1]
+                        block[v][o] = acc
+        rest = [r for r in range(12) if r // 4 != a]
         for v in range(V):
-            for b in range(12):
-                if b == r:
-                    continue
-                src = mats[v][b]
-                acc = src
-                for i in pivots:
-                    p = 8 * r + i
-                    colb = jnp.broadcast_to(src[:, p : p + 1], (8, 128))
-                    acc = acc - colb * panel[v][i : i + 1, :]
-                mats[v][b] = acc
-            mats[v][r] = panel[v]
+            for q in range(4):
+                mats[v][4 * a + q] = block[v][q]
+            solved = jnp.concatenate(block[v][:3] + [jnp.where(sub == 7, 0.0, block[v][3])], axis=0)
+            zero = jnp.zeros((32, 128), F32)
+            factor = jnp.concatenate([solved if t == a else zero for t in range(4)], axis=0)
+            old = jnp.concatenate([mats[v][r] for r in rest], axis=0)
+            upd = old - jnp.dot(old, factor, preferred_element_type=F32, precision=lax.Precision.HIGHEST)
+            for n, r in enumerate(rest):
+                mats[v][r] = upd[8 * n : 8 * n + 8]
 
     row_coord = (lax.broadcasted_iota(jnp.int32, (8, 128), 0).astype(F32) + 0.5 - 64.0) / 64.0
     col_coord = (lane.astype(F32) + 0.5 - 64.0) / 64.0
@@ -300,7 +327,7 @@
             pltpu.VMEM((V, 4, 32, 128), F32),
             pltpu.VMEM((V, TH, TW), F32),
         ],
-        compiler_params=pltpu.CompilerParams(vmem_limit_bytes=56 * 1024 * 1024),
+        compiler_params=pltpu.CompilerParams(vmem_limit_bytes=20 * 1024 * 1024),
         name="fit",
     )(dither, stamps, mid, left, right, science, mask,
       jnp.asarray(column_matrix(table)), jnp.asarray(row_matrix(table)))

time: 85.3 us -> 74.5 us (0.87)
  Pallas kernels: 30.9 us -> 19.7 us
    pallas_call x1, Pallas kernels: 30.9 us -> 19.7 us  [fit_kernel(): pl.pallas_call(body, out_shape=(jax.ShapeDtypeStruct((V, TH, TW), F32), j...]
    mul x1, other arithmetic: 1.84 us -> 0.82 us  [on_device(): return diff * lax.rsqrt(noise + var + 1e-06)]
    concatenate x1, other arithmetic: 0.03 us -> 0.9 us  [on_device(): mid = jnp.concatenate([above, planes, below], axis=1)]
  transfers between devices with their start and end apart: 9 -> 9, of which waited for: 8 -> 8; matrix products, arithmetic and copies ran while one was open for 1% -> 0% of each run, Pallas kernels for 0% -> 0%
where the time goes in v2:
time: 74.5 us; the launch traced here: 74.2 us
  starting transfers between devices  35.6 us (48%)
  Pallas kernels  19.7 us (26%)
  waiting for transfers between devices  13.8 us (19%)
  other arithmetic  2.8 us (4%)
  local copies, waits for them, and re-layouts  2.15 us (3%)
    ppermute x5, starting transfers between devices, strip_sum(): lax.ppermute(x, 'fcol', [(i, i ^ k) for i in range(lax.axis_size('fcol'))])  25.3 us
    pallas_call x1, Pallas kernels, fit_kernel(): pl.pallas_call(body, out_shape=(jax.ShapeDtypeStruct((V, TH, TW), F32), j...  19.7 us
    ppermute x4, starting transfers between devices, shift(): lax.ppermute(x, axis, [(i, i + step) for i in range(count) if 0 <= i + st...  10.3 us
    ppermute x5, waiting for transfers between devices, strip_sum(): lax.ppermute(x, 'fcol', [(i, i ^ k) for i in range(lax.axis_size('fcol'))])  7.16 us
    ppermute x4, waiting for transfers between devices, shift(): lax.ppermute(x, axis, [(i, i + step) for i in range(count) if 0 <= i + st...  6.69 us
    unnamed x13, local copies, waits for them, and re-layouts  2.15 us
  transfers between devices with their start and end apart: 9, of which 8 were waited for; matrix products, arithmetic and copies ran while one was open for 0% of the time, Pallas kernels for 0%

profile of v2, /device:TPU:24, one launch (start us, length us, event | category | flops | bytes accessed | tf_op | source)
XLA Modules:
  0.0 74.2 jit_solution(12303931567770176102)
XLA Ops:
  0.0 0.0 copy-start
  0.0 1.0 %pad_maximum_fusion.1 = f32[2,128,128]{2,1,0:T(8,128)S(1)} fusion(f32[1,128,128]{2,1,0:T(8,128)} %bitcast.4, f32[1,128,128]{2,1,0:T(8,128)} %bitcast.6), kind=kLoop, calls=%fused_computation.2 | loop fusion | flops 32768 | bytes 262144 | tf_op jit(solution)/shard_map/stack | solution.py:350
  1.0 0.0 copy-start.5
  1.0 0.0 copy-start.2
  1.0 3.7 %collective-permute-start.1 = (f32[2,128,128]{2,1,0:T(8,128)S(1)}, f32[2,128,128]{2,1,0:T(8,128)S(1)}, u32[]{:S(2)}, u32[]{:S(2)}) collective-permute-start(f32[2,128,128]{2,1,0:T(8,128)S(1)} %pad_maximum_fusion.1), channel_id=1, source_target_pairs={{32,0},{64,32},{96,64},{128,96},{160,128},{192,160},{224,192},{33,... | collective-permute-start | bytes 393224 | tf_op jit(solution)/shard_map/ppermute | solution.py:338
  4.7 2.3 %collective-permute-start = (f32[2,128,128]{2,1,0:T(8,128)S(1)}, f32[2,128,128]{2,1,0:T(8,128)S(1)}, u32[]{:S(2)}, u32[]{:S(2)}) collective-permute-start(f32[2,128,128]{2,1,0:T(8,128)S(1)} %pad_maximum_fusion.1), channel_id=1, source_target_pairs={{0,32},{32,64},{64,96},{96,128},{128,160},{160,192},{192,224},{1,3... | collective-permute-start | bytes 393224 | tf_op jit(solution)/shard_map/ppermute | solution.py:338
  7.0 1.3 %collective-permute-done.1 = f32[2,128,128]{2,1,0:T(8,128)S(1)} collective-permute-done((f32[2,128,128]{2,1,0:T(8,128)S(1)}, f32[2,128,128]{2,1,0:T(8,128)S(1)}, u32[]{:S(2)}, u32[]{:S(2)}) %collective-permute-start.1) | collective-permute-done | bytes 131104 | tf_op jit(solution)/shard_map/ppermute | solution.py:338
  8.2 4.2 %collective-permute-done = f32[2,128,128]{2,1,0:T(8,128)S(1)} collective-permute-done((f32[2,128,128]{2,1,0:T(8,128)S(1)}, f32[2,128,128]{2,1,0:T(8,128)S(1)}, u32[]{:S(2)}, u32[]{:S(2)}) %collective-permute-start) | collective-permute-done | bytes 131104 | tf_op jit(solution)/shard_map/ppermute | solution.py:338
  12.5 0.9 %pad_maximum_fusion.mid = f32[2,384,128]{2,1,0:T(8,128)S(1)} fusion(f32[2,128,128]{2,1,0:T(8,128)S(1)} %collective-permute-done.1, f32[1,128,128]{2,1,0:T(8,128)} %bitcast.5, f32[1,128,128]{2,1,0:T(8,128)} %bitcast.7, f32[2,128,128]{2,1,0:T(8,128)S(1)} %collective-permute-done), kind=kLoop, calls=%fused_computation | loop fusion | flops 294912 | bytes 786432 | tf_op jit(solution)/shard_map/concatenate | solution.py:353
  13.4 0.0 copy-start.4
  13.4 1.3 %collective-permute-start.3 = (f32[2,384,128]{2,1,0:T(8,128)S(1)}, f32[2,384,128]{2,1,0:T(8,128)S(1)}, u32[]{:S(2)}, u32[]{:S(2)}) collective-permute-start(f32[2,384,128]{2,1,0:T(8,128)S(1)} %pad_maximum_fusion.mid), channel_id=1, source_target_pairs={{1,0},{2,1},{3,2},{4,3},{5,4},{6,5},{7,6},{8,7},{9,8},{10,9},{11,1... | collective-permute-start | bytes 1179656 | tf_op jit(solution)/shard_map/ppermute | solution.py:338
  14.7 3.1 %collective-permute-start.2 = (f32[2,384,128]{2,1,0:T(8,128)S(1)}, f32[2,384,128]{2,1,0:T(8,128)S(1)}, u32[]{:S(2)}, u32[]{:S(2)}) collective-permute-start(f32[2,384,128]{2,1,0:T(8,128)S(1)} %pad_maximum_fusion.mid), channel_id=1, source_target_pairs={{0,1},{1,2},{2,3},{3,4},{4,5},{5,6},{6,7},{7,8},{8,9},{9,10},{10,1... | collective-permute-start | bytes 1179656 | tf_op jit(solution)/shard_map/ppermute | solution.py:338
  17.7 0.0 copy-done.5
  17.8 0.1 copy.10.dither
  17.8 0.0 collective-permute-done.3.right
  17.8 1.2 %collective-permute-done.2.left = f32[2,384,128]{2,1,0:T(8,128)S(1)} collective-permute-done((f32[2,384,128]{2,1,0:T(8,128)S(1)}, f32[2,384,128]{2,1,0:T(8,128)S(1)}, u32[]{:S(2)}, u32[]{:S(2)}) %collective-permute-start.2) | collective-permute-done | bytes 393248 | tf_op jit(solution)/shard_map/ppermute | solution.py:338
  19.0 0.0 copy-done
  19.1 0.0 copy-done.2
  19.1 0.0 copy-done.4
  19.1 0.0 copy-start.1
  19.1 1.1 %copy-done.1 = bf16[512,608]{1,0:T(8,128)(2,1)S(1)} copy-done((bf16[512,608]{1,0:T(8,128)(2,1)S(1)}, bf16[512,608]{1,0:T(8,128)(2,1)}, u32[]{:S(2)}) %copy-start.1) | copy-done | bytes 622616
  20.1 0.0 copy-start.3
  20.1 0.9 %copy-done.3 = s32[4,128,128]{2,1,0:T(8,128)S(1)} copy-done((s32[4,128,128]{2,1,0:T(8,128)S(1)}, s32[4,128,128]{2,1,0:T(8,128)}, u32[]{:S(2)}) %copy-start.3) | copy-done | bytes 262168
  21.1 19.7 %fit.1 = (f32[4,128,128]{2,1,0:T(8,128)S(1)}, f32[4,128,128]{2,1,0:T(8,128)S(1)}, f32[8,128]{1,0:T(8,128)S(1)}) custom-call(s32[4,2]{1,0:T(4,128)S(1)} %copy.10.dither, s32[4,12]{1,0:T(4,128)S(1)} %bitcast.3, f32[2,384,128]{2,1,0:T(8,128)S(1)} %pad_maximum_fusion.mid, f32[2,384,128]{2,1,0:T(8,128)S(1)} %collective-permute-done.2.left, ...), custom_call_target="tpu_custom_call" | custom-call | tf_op jit(solution)/shard_map/fit/pallas_call | solution.py:313
  40.8 7.5 %collective-permute-start.4 = (f32[8,128]{1,0:T(8,128)S(1)}, f32[8,128]{1,0:T(8,128)S(1)}, u32[]{:S(2)}, u32[]{:S(2)}) collective-permute-start(f32[8,128]{1,0:T(8,128)S(1)} %get-tuple-element.9), channel_id=1, source_target_pairs={{0,1},{1,0},{2,3},{3,2},{4,5},{5,4},{6,7},{7,6},{8,9},{9,8},{10,11... | collective-permute-start | bytes 12296 | tf_op jit(solution)/shard_map/ppermute | solution.py:345
  48.3 0.8 %collective-permute-done.4 = f32[8,128]{1,0:T(8,128)S(1)} collective-permute-done((f32[8,128]{1,0:T(8,128)S(1)}, f32[8,128]{1,0:T(8,128)S(1)}, u32[]{:S(2)}, u32[]{:S(2)}) %collective-permute-start.4) | collective-permute-done | bytes 4128 | tf_op jit(solution)/shard_map/ppermute | solution.py:345
  49.1 4.2 %collective-permute-start.5 = (f32[8,128]{1,0:T(8,128)S(1)}, f32[8,128]{1,0:T(8,128)S(1)}, u32[]{:S(2)}, u32[]{:S(2)}) collective-permute-start(f32[8,128]{1,0:T(8,128)S(1)} %add.29), channel_id=1, source_target_pairs={{0,2},{1,3},{2,0},{3,1},{4,6},{5,7},{6,4},{7,5},{8,10},{9,11},{10,... | collective-permute-start | bytes 12296 | tf_op jit(solution)/shard_map/ppermute | solution.py:345
  53.3 1.6 %collective-permute-done.5 = f32[8,128]{1,0:T(8,128)S(1)} collective-permute-done((f32[8,128]{1,0:T(8,128)S(1)}, f32[8,128]{1,0:T(8,128)S(1)}, u32[]{:S(2)}, u32[]{:S(2)}) %collective-permute-start.5) | collective-permute-done | bytes 4128 | tf_op jit(solution)/shard_map/ppermute | solution.py:345
  54.9 2.5 %collective-permute-start.6 = (f32[8,128]{1,0:T(8,128)S(1)}, f32[8,128]{1,0:T(8,128)S(1)}, u32[]{:S(2)}, u32[]{:S(2)}) collective-permute-start(f32[8,128]{1,0:T(8,128)S(1)} %add.30), channel_id=1, source_target_pairs={{0,4},{1,5},{2,6},{3,7},{4,0},{5,1},{6,2},{7,3},{8,12},{9,13},{10,... | collective-permute-start | bytes 12296 | tf_op jit(solution)/shard_map/ppermute | solution.py:345
  57.4 1.6 %collective-permute-done.6 = f32[8,128]{1,0:T(8,128)S(1)} collective-permute-done((f32[8,128]{1,0:T(8,128)S(1)}, f32[8,128]{1,0:T(8,128)S(1)}, u32[]{:S(2)}, u32[]{:S(2)}) %collective-permute-start.6) | collective-permute-done | bytes 4128 | tf_op jit(solution)/shard_map/ppermute | solution.py:345
  59.0 3.9 %collective-permute-start.7 = (f32[8,128]{1,0:T(8,128)S(1)}, f32[8,128]{1,0:T(8,128)S(1)}, u32[]{:S(2)}, u32[]{:S(2)}) collective-permute-start(f32[8,128]{1,0:T(8,128)S(1)} %add.31), channel_id=1, source_target_pairs={{0,8},{1,9},{2,10},{3,11},{4,12},{5,13},{6,14},{7,15},{8,0},{9,1},... | collective-permute-start | bytes 12296 | tf_op jit(solution)/shard_map/ppermute | solution.py:345
  62.9 1.6 %collective-permute-done.7 = f32[8,128]{1,0:T(8,128)S(1)} collective-permute-done((f32[8,128]{1,0:T(8,128)S(1)}, f32[8,128]{1,0:T(8,128)S(1)}, u32[]{:S(2)}, u32[]{:S(2)}) %collective-permute-start.7) | collective-permute-done | bytes 4128 | tf_op jit(solution)/shard_map/ppermute | solution.py:345
  64.5 7.1 %collective-permute-start.8 = (f32[8,128]{1,0:T(8,128)S(1)}, f32[8,128]{1,0:T(8,128)S(1)}, u32[]{:S(2)}, u32[]{:S(2)}) collective-permute-start(f32[8,128]{1,0:T(8,128)S(1)} %add.32), channel_id=1, source_target_pairs={{0,16},{1,17},{2,18},{3,19},{4,20},{5,21},{6,22},{7,23},{8,24},{9,... | collective-permute-start | bytes 12296 | tf_op jit(solution)/shard_map/ppermute | solution.py:345
  71.6 1.6 %collective-permute-done.8 = f32[8,128]{1,0:T(8,128)S(1)} collective-permute-done((f32[8,128]{1,0:T(8,128)S(1)}, f32[8,128]{1,0:T(8,128)S(1)}, u32[]{:S(2)}, u32[]{:S(2)}) %collective-permute-start.8) | collective-permute-done | bytes 4128 | tf_op jit(solution)/shard_map/ppermute | solution.py:345
  73.2 0.1 multiply_reduce_fusion
  73.3 0.8 %rsqrt_multiply_fusion = f32[4,128,128]{2,1,0:T(8,128)} fusion(f32[4,128,128]{2,1,0:T(8,128)S(1)} %get-tuple-element.8, f32[4,128,128]{2,1,0:T(8,128)S(1)} %get-tuple-element.10, f32[4]{0:T(128)S(1)} %multiply_reduce_fusion), kind=kLoop, calls=%fused_computation.1 | loop fusion | flops 196608 | bytes 786448 | tf_op jit(solution)/shard_map/mul | solution.py:362
  (5 shorter events, 0.0 us)
Async XLA Ops:
  0.0 19.0 %copy-start = (bf16[256,1536]{1,0:T(8,128)(2,1)S(1)}, bf16[256,1536]{1,0:T(8,128)(2,1)}, u32[]{:S(2)}) copy-start(bf16[256,1536]{1,0:T(8,128)(2,1)} %constant.9.clone.tcol) | copy-start | bytes 2359300
  1.0 16.8 %copy-start.5 = (s32[4,2]{0,1:T(2,128)S(1)}, s32[4,2]{0,1:T(2,128)}, u32[]{:S(2)}) copy-start(s32[4,2]{0,1:T(2,128)} %param.12) | copy-start | bytes 100
  1.0 18.1 %copy-start.2 = (f32[4,128,128]{2,1,0:T(8,128)S(1)}, f32[4,128,128]{2,1,0:T(8,128)}, u32[]{:S(2)}) copy-start(f32[4,128,128]{2,1,0:T(8,128)} %science.1) | copy-start | bytes 786436
  1.0 7.3 %collective-permute-start.1 = (f32[2,128,128]{2,1,0:T(8,128)S(1)}, f32[2,128,128]{2,1,0:T(8,128)S(1)}, u32[]{:S(2)}, u32[]{:S(2)}) collective-permute-start(f32[2,128,128]{2,1,0:T(8,128)S(1)} %pad_maximum_fusion.1), channel_id=1, source_target_pairs={{32,0},{64,32},{96,64},{128,96},{160,128},{192,160},{224,192},{33,... | collective-permute-start | bytes 393224 | tf_op jit(solution)/shard_map/ppermute | solution.py:338
  4.7 7.8 %collective-permute-start = (f32[2,128,128]{2,1,0:T(8,128)S(1)}, f32[2,128,128]{2,1,0:T(8,128)S(1)}, u32[]{:S(2)}, u32[]{:S(2)}) collective-permute-start(f32[2,128,128]{2,1,0:T(8,128)S(1)} %pad_maximum_fusion.1), channel_id=1, source_target_pairs={{0,32},{32,64},{64,96},{96,128},{128,160},{160,192},{192,224},{1,3... | collective-permute-start | bytes 393224 | tf_op jit(solution)/shard_map/ppermute | solution.py:338
  13.4 5.7 %copy-start.4 = (s32[4,1,1,12]{3,2,1,0:T(1,128)S(1)}, s32[4,1,1,12]{3,2,1,0:T(1,128)}, u32[]{:S(2)}) copy-start(s32[4,1,1,12]{3,2,1,0:T(1,128)} %param.13) | copy-start | bytes 580
  13.4 4.5 %collective-permute-start.3 = (f32[2,384,128]{2,1,0:T(8,128)S(1)}, f32[2,384,128]{2,1,0:T(8,128)S(1)}, u32[]{:S(2)}, u32[]{:S(2)}) collective-permute-start(f32[2,384,128]{2,1,0:T(8,128)S(1)} %pad_maximum_fusion.mid), channel_id=1, source_target_pairs={{1,0},{2,1},{3,2},{4,3},{5,4},{6,5},{7,6},{8,7},{9,8},{10,9},{11,1... | collective-permute-start | bytes 1179656 | tf_op jit(solution)/shard_map/ppermute | solution.py:338
  14.7 4.4 %collective-permute-start.2 = (f32[2,384,128]{2,1,0:T(8,128)S(1)}, f32[2,384,128]{2,1,0:T(8,128)S(1)}, u32[]{:S(2)}, u32[]{:S(2)}) collective-permute-start(f32[2,384,128]{2,1,0:T(8,128)S(1)} %pad_maximum_fusion.mid), channel_id=1, source_target_pairs={{0,1},{1,2},{2,3},{3,4},{4,5},{5,6},{6,7},{7,8},{8,9},{9,10},{10,1... | collective-permute-start | bytes 1179656 | tf_op jit(solution)/shard_map/ppermute | solution.py:338
  19.1 1.1 %copy-start.1 = (bf16[512,608]{1,0:T(8,128)(2,1)S(1)}, bf16[512,608]{1,0:T(8,128)(2,1)}, u32[]{:S(2)}) copy-start(bf16[512,608]{1,0:T(8,128)(2,1)} %constant.10.clone.trow) | copy-start | bytes 1867780
  20.1 0.9 %copy-start.3 = (s32[4,128,128]{2,1,0:T(8,128)S(1)}, s32[4,128,128]{2,1,0:T(8,128)}, u32[]{:S(2)}) copy-start(s32[4,128,128]{2,1,0:T(8,128)} %mask.1) | copy-start | bytes 786436
  40.8 8.3 %collective-permute-start.4 = (f32[8,128]{1,0:T(8,128)S(1)}, f32[8,128]{1,0:T(8,128)S(1)}, u32[]{:S(2)}, u32[]{:S(2)}) collective-permute-start(f32[8,128]{1,0:T(8,128)S(1)} %get-tuple-element.9), channel_id=1, source_target_pairs={{0,1},{1,0},{2,3},{3,2},{4,5},{5,4},{6,7},{7,6},{8,9},{9,8},{10,11... | collective-permute-start | bytes 12296 | tf_op jit(solution)/shard_map/ppermute | solution.py:345
  49.1 5.8 %collective-permute-start.5 = (f32[8,128]{1,0:T(8,128)S(1)}, f32[8,128]{1,0:T(8,128)S(1)}, u32[]{:S(2)}, u32[]{:S(2)}) collective-permute-start(f32[8,128]{1,0:T(8,128)S(1)} %add.29), channel_id=1, source_target_pairs={{0,2},{1,3},{2,0},{3,1},{4,6},{5,7},{6,4},{7,5},{8,10},{9,11},{10,... | collective-permute-start | bytes 12296 | tf_op jit(solution)/shard_map/ppermute | solution.py:345
  54.9 4.1 %collective-permute-start.6 = (f32[8,128]{1,0:T(8,128)S(1)}, f32[8,128]{1,0:T(8,128)S(1)}, u32[]{:S(2)}, u32[]{:S(2)}) collective-permute-start(f32[8,128]{1,0:T(8,128)S(1)} %add.30), channel_id=1, source_target_pairs={{0,4},{1,5},{2,6},{3,7},{4,0},{5,1},{6,2},{7,3},{8,12},{9,13},{10,... | collective-permute-start | bytes 12296 | tf_op jit(solution)/shard_map/ppermute | solution.py:345
  59.0 5.5 %collective-permute-start.7 = (f32[8,128]{1,0:T(8,128)S(1)}, f32[8,128]{1,0:T(8,128)S(1)}, u32[]{:S(2)}, u32[]{:S(2)}) collective-permute-start(f32[8,128]{1,0:T(8,128)S(1)} %add.31), channel_id=1, source_target_pairs={{0,8},{1,9},{2,10},{3,11},{4,12},{5,13},{6,14},{7,15},{8,0},{9,1},... | collective-permute-start | bytes 12296 | tf_op jit(solution)/shard_map/ppermute | solution.py:345
  64.5 8.7 %collective-permute-start.8 = (f32[8,128]{1,0:T(8,128)S(1)}, f32[8,128]{1,0:T(8,128)S(1)}, u32[]{:S(2)}, u32[]{:S(2)}) collective-permute-start(f32[8,128]{1,0:T(8,128)S(1)} %add.32), channel_id=1, source_target_pairs={{0,16},{1,17},{2,18},{3,19},{4,20},{5,21},{6,22},{7,23},{8,24},{9,... | collective-permute-start | bytes 12296 | tf_op jit(solution)/shard_map/ppermute | solution.py:345

commit v3 on v2

--- a/solution.py
+++ b/solution.py
@@ -73,11 +73,15 @@
     return pltpu.roll(x, shift, 1)
 
 
-def body(dither, stamps, mid, left, right, science, mask, tcol, trow, diff_out, var_out, tot_out,
-         planes, cbuf, sbuf, dbuf, gbuf, wbuf):
+def body(dither, stamps, parity, mid, side_a, side_b, visits, tables,
+         diff_out, var_out, tot_out, planes, cbuf, sbuf, dbuf, gbuf, wbuf):
+    row_a = pl.multiple_of(parity[0] * 256, 128)
+    row_b = pl.multiple_of(256 - parity[0] * 256, 128)
     for p in range(2):
-        for b, ref in ((0, left), (1, mid), (2, right)):
-            planes[p, b, 0:384, :] = ref[p]
+        for b, ref in ((1, mid), (2 * parity[1], side_a), (2 - 2 * parity[1], side_b)):
+            planes[p, b, pl.ds(row_a, 128), :] = ref[p, 0:128, :]
+            planes[p, b, 128:256, :] = ref[p, 128:256, :]
+            planes[p, b, pl.ds(row_b, 128), :] = ref[p, 256:384, :]
             planes[p, b, 384:PROWS, :] = jnp.zeros((PROWS - 384, 128), F32)
     lane = lax.broadcasted_iota(jnp.int32, (8, 128), 1)
     sub = lax.broadcasted_iota(jnp.int32, (8, 128), 0)
@@ -109,12 +113,11 @@
         q1 = roll_lanes(planes[1, nxt, pl.ds(MARGIN + dy, TH), :], back1)
         var = jnp.where(lane1 < 128 - s1, q0, q1)
         var_out[v] = var
-        usable = (mask[v] == 0).astype(F32)
-        wbuf[v] = usable / (0.25 + var)
-        sbuf[:, v * TW : (v + 1) * TW] = science[v].astype(BF)
-
-    for v in range(V):
-        cp = jnp.dot(windows[v], tcol[...], preferred_element_type=F32).astype(BF)
+        wbuf[v] = visits[V + v] / (0.25 + var)
+        sbuf[:, v * TW : (v + 1) * TW] = visits[v].astype(BF)
+
+    for v in range(V):
+        cp = jnp.dot(windows[v], tables[0:256, :], preferred_element_type=F32).astype(BF)
         for f in range(F):
             cbuf[f, :, v * TW : (v + 1) * TW] = cp[:, f * TW : (f + 1) * TW]
 
@@ -127,36 +130,36 @@
             + [sbuf[pl.ds(base, YB), :], ones_piece],
             axis=0,
         )
-        out = jnp.dot(trow[...], slab, preferred_element_type=F32).astype(BF)
+        trow = jnp.concatenate([tables[256:512, 0:KDIM], tables[256:512, 640 : 640 + KDIM]], axis=0)
+        out = jnp.dot(trow, slab, preferred_element_type=F32).astype(BF)
         dbuf[pl.ds(pl.multiple_of(yb * (YB * 32), YB * 32), YB * 32), :] = out
         return carry
 
     lax.fori_loop(0, TH // YB, row_block, 0)
 
-    group_masks = [
-        ((lax.broadcasted_iota(jnp.int32, (32, 128), 1) // 32) == j).astype(F32).astype(BF)
-        for j in range(4)
-    ]
+    lanes32 = lax.broadcasted_iota(jnp.int32, (32, 128), 1)
+    half_masks = [(lanes32 // 64 == h).astype(F32) for h in range(2)]
+    odd_masks = [((lanes32 // 32) % 2 == h).astype(F32).astype(BF) for h in range(2)]
     for v in range(V):
 
         def gram_row(i, carry, v=v):
-            acc = jnp.zeros((32, 128), F32)
+            acc = jnp.zeros((64, 64), F32)
             for c in range(8):
                 ws = []
-                ds = [[] for _ in range(4)]
+                ds = []
                 for t in range(4):
                     y = i * 32 + c * 4 + t
                     d = dbuf[pl.ds(pl.multiple_of(y * 32, 32), 32), v * TW : (v + 1) * TW]
-                    w = wbuf[v, pl.ds(y, 1), :]
-                    ws.append((d.astype(F32) * w).astype(BF))
-                    for j in range(4):
-                        ds[j].append(d * group_masks[j])
-                wcat = jnp.concatenate(ws, axis=1)
-                dcat = jnp.concatenate([jnp.concatenate(q, axis=1) for q in ds], axis=0)
+                    w = d.astype(F32) * wbuf[v, pl.ds(y, 1), :]
+                    ws.append(jnp.concatenate([(w * m).astype(BF) for m in half_masks], axis=0))
+                    ds.append(jnp.concatenate([d * m for m in odd_masks], axis=0))
                 acc = acc + lax.dot_general(
-                    wcat, dcat, (((1,), (1,)), ((), ())), preferred_element_type=F32
+                    jnp.concatenate(ws, axis=1),
+                    jnp.concatenate(ds, axis=1),
+                    (((1,), (1,)), ((), ())),
+                    preferred_element_type=F32,
                 )
-            gbuf[v, i] = acc
+            gbuf[v, i] = jnp.concatenate([acc[:32], acc[32:]], axis=1)
             return carry
 
         lax.fori_loop(0, 4, gram_row, 0)
@@ -296,9 +299,9 @@
             o = o[:24] + o[24:]
             model = o[0:8] + col_coord * o[8:16] + (row_coord + yb / 8.0) * o[16:24]
             rows8 = pl.ds(yb * 8, 8)
-            diff = science[v, rows8, :] - model
+            diff = visits[v, rows8, :] - model
             diff_out[v, rows8, :] = diff
-            total = total + jnp.where(mask[v, rows8, :] == 0, diff * diff, 0.0)
+            total = total + visits[V + v, rows8, :] * (diff * diff)
         tot_rows.append(jnp.sum(total, axis=0, keepdims=True))
     tot_rows += [jnp.zeros((1, 128), F32)] * 4
     tot_out[...] = jnp.broadcast_to(
@@ -306,10 +309,15 @@
     )
 
 
-def fit_kernel(dither, stamps, mid, left, right, science, mask):
+def fit_kernel(dither, stamps, parity, mid, side_a, side_b, visits):
     table = kernel_table()
     vmem = pl.BlockSpec(memory_space=pltpu.VMEM)
     smem = pl.BlockSpec(memory_space=pltpu.SMEM)
+    tables = np.zeros((512, F * TW), BF)
+    tables[0:256] = column_matrix(table)
+    rows = row_matrix(table)
+    tables[256:512, 0:KDIM] = rows[0:256]
+    tables[256:512, 640 : 640 + KDIM] = rows[256:512]
     return pl.pallas_call(
         body,
         out_shape=(
@@ -317,7 +325,7 @@
             jax.ShapeDtypeStruct((V, TH, TW), F32),
             jax.ShapeDtypeStruct((8, 128), F32),
         ),
-        in_specs=[smem, smem] + [vmem] * 7,
+        in_specs=[smem] * 3 + [vmem] * 5,
         out_specs=(vmem, vmem, vmem),
         scratch_shapes=[
             pltpu.VMEM((2, 3, PROWS, 128), F32),
@@ -329,36 +337,38 @@
         ],
         compiler_params=pltpu.CompilerParams(vmem_limit_bytes=20 * 1024 * 1024),
         name="fit",
-    )(dither, stamps, mid, left, right, science, mask,
-      jnp.asarray(column_matrix(table)), jnp.asarray(row_matrix(table)))
-
-
-def shift(x, axis, step):
-    count = lax.axis_size(axis)
-    return lax.ppermute(
-        x, axis, [(i, i + step) for i in range(count) if 0 <= i + step < count]
+    )(dither, stamps, parity, mid, side_a, side_b, visits, jnp.asarray(tables))
+
+
+def exchange(x, axis, first):
+    pairs = []
+    for i in range(first, lax.axis_size(axis) - 1, 2):
+        pairs += [(i, i + 1), (i + 1, i)]
+    return lax.ppermute(x, axis, pairs)
+
+
+def strip_sum(x):
+    count = lax.axis_size("fcol")
+    parts = jnp.broadcast_to(x[None, :], (count, x.shape[0]))
+    return jnp.sum(lax.all_to_all(parts, "fcol", 0, 0, tiled=True), axis=0)
+
+
+def on_device(science, pixel_mask, coadd_image, coadd_variance, dither, stamps):
+    parity = jnp.bitwise_and(jnp.stack([lax.axis_index("frow"), lax.axis_index("fcol")]), 1)
+    planes = lax.optimization_barrier(jnp.stack([coadd_image, coadd_variance]))
+    rows_a = exchange(planes, "frow", 1)
+    rows_b = exchange(planes, "frow", 0)
+    mid = jnp.concatenate([rows_a, planes, rows_b], axis=1)
+    mid, science, pixel_mask = lax.optimization_barrier((mid, science, pixel_mask))
+    visits = jnp.concatenate([science, (pixel_mask == 0).astype(F32)], axis=0)
+    side_b = exchange(mid, "fcol", 0)
+    side_a = exchange(mid, "fcol", 1)
+    diff, var, tot = fit_kernel(
+        dither, stamps.reshape(V, SMAX), parity, mid, side_a, side_b, visits
     )
-
-
-def strip_sum(x):
-    for k in (1, 2, 4, 8, 16):
-        x = x + lax.ppermute(x, "fcol", [(i, i ^ k) for i in range(lax.axis_size("fcol"))])
-    return x
-
-
-def on_device(science, pixel_mask, coadd_image, coadd_variance, dither, stamps):
-    planes = jnp.stack([coadd_image, coadd_variance])
-    above = shift(planes, "frow", 1)
-    below = shift(planes, "frow", -1)
-    mid = jnp.concatenate([above, planes, below], axis=1)
-    left = shift(mid, "fcol", 1)
-    right = shift(mid, "fcol", -1)
-    diff, var, tot = fit_kernel(
-        dither, stamps.reshape(V, SMAX), mid, left, right, science, pixel_mask
-    )
-    tot = strip_sum(tot)
+    tot = strip_sum(tot[:V, 0])
     pixel_count = TH * TW * lax.axis_size("fcol")
-    noise = tot[:V, :1].reshape(V, 1, 1) / pixel_count
+    noise = tot.reshape(V, 1, 1) / pixel_count
     return diff * lax.rsqrt(noise + var + 1e-06)
 
 

time: 74.5 us -> 65.3 us (0.88)
  blocking collectives: 0 us -> 31.9 us
  starting transfers between devices: 35.6 us -> 4.97 us
  waiting for transfers between devices: 13.8 us -> 5.13 us
  Pallas kernels: 19.7 us -> 18.1 us
  local copies, waits for them, and re-layouts: 2.15 us -> 0.9 us
  other arithmetic: 2.8 us -> 3.94 us
    all_to_all x0 -> x1, blocking collectives: none -> 31.9 us  [strip_sum(): return jnp.sum(lax.all_to_all(parts, 'fcol', 0, 0, tiled=True), axis=0)]
    ppermute x9 -> x4, starting transfers between devices: 35.6 us -> 4.97 us  [exchange(): return lax.ppermute(x, axis, pairs)]
    ppermute x9 -> x4, waiting for transfers between devices: 13.8 us -> 5.13 us  [exchange(): return lax.ppermute(x, axis, pairs)]
    pallas_call x1, Pallas kernels: 19.7 us -> 18.1 us  [fit_kernel(): pl.pallas_call(body, out_shape=(jax.ShapeDtypeStruct((V, TH, TW), F32), j...]
    unnamed x13 -> x5, local copies, waits for them, and re-layouts: 2.15 us -> 0.77 us
    convert_element_type x0 -> x1, other arithmetic: none -> 0.97 us  [on_device(): visits = jnp.concatenate([science, (pixel_mask == 0).astype(F32)], axis=0)]
  transfers between devices with their start and end apart: 9 -> 4, of which waited for: 8 -> 2; matrix products, arithmetic and copies ran while one was open for 0% -> 4% of each run, Pallas kernels for 0% -> 0%
where the time goes in v3:
time: 65.3 us; the launch traced here: 65 us
  blocking collectives  31.9 us (49%)
  Pallas kernels  18.1 us (28%)
  waiting for transfers between devices  5.13 us (8%)
  starting transfers between devices  4.97 us (8%)
  other arithmetic  3.94 us (6%)
  local copies, waits for them, and re-layouts  0.9 us (1%)
    all_to_all x1, blocking collectives, strip_sum(): return jnp.sum(lax.all_to_all(parts, 'fcol', 0, 0, tiled=True), axis=0)  31.9 us
    pallas_call x1, Pallas kernels, fit_kernel(): pl.pallas_call(body, out_shape=(jax.ShapeDtypeStruct((V, TH, TW), F32), j...  18.1 us
    ppermute x4, waiting for transfers between devices, exchange(): return lax.ppermute(x, axis, pairs)  5.13 us
    ppermute x4, starting transfers between devices, exchange(): return lax.ppermute(x, axis, pairs)  4.97 us
  transfers between devices with their start and end apart: 4, of which 2 were waited for; matrix products, arithmetic and copies ran while one was open for 4% of the time, Pallas kernels for 0%

profile of v3, /device:TPU:24, one launch (start us, length us, event | category | flops | bytes accessed | tf_op | source)
XLA Modules:
  0.0 65.0 jit_solution(10762511183722563538)
XLA Ops:
  0.0 0.0 copy-start
  0.0 0.0 copy-start.1
  0.0 1.0 %pad_maximum_fusion.2 = f32[2,128,128]{2,1,0:T(8,128)S(1)} fusion(f32[1,128,128]{2,1,0:T(8,128)} %bitcast.6, f32[1,128,128]{2,1,0:T(8,128)} %bitcast.7), kind=kLoop, calls=%fused_computation.4 | loop fusion | flops 32768 | bytes 262144 | tf_op jit(solution)/shard_map/stack | solution.py:358
  1.0 1.6 %collective-permute-start.1 = (f32[2,128,128]{2,1,0:T(8,128)S(1)}, f32[2,128,128]{2,1,0:T(8,128)S(1)}, u32[]{:S(2)}, u32[]{:S(2)}) collective-permute-start(f32[2,128,128]{2,1,0:T(8,128)S(1)} %pad_maximum_fusion.2), channel_id=1, source_target_pairs={{0,32},{32,0},{64,96},{96,64},{128,160},{160,128},{192,224},{224,1... | collective-permute-start | bytes 393224 | tf_op jit(solution)/shard_map/ppermute | solution.py:347
  2.6 2.6 %collective-permute-start = (f32[2,128,128]{2,1,0:T(8,128)S(1)}, f32[2,128,128]{2,1,0:T(8,128)S(1)}, u32[]{:S(2)}, u32[]{:S(2)}) collective-permute-start(f32[2,128,128]{2,1,0:T(8,128)S(1)} %pad_maximum_fusion.2), channel_id=1, source_target_pairs={{32,64},{64,32},{96,128},{128,96},{160,192},{192,160},{33,65},{65,... | collective-permute-start | bytes 393224 | tf_op jit(solution)/shard_map/ppermute | solution.py:347
  5.2 1.1 %collective-permute-done.1 = f32[2,128,128]{2,1,0:T(8,128)S(1)} collective-permute-done((f32[2,128,128]{2,1,0:T(8,128)S(1)}, f32[2,128,128]{2,1,0:T(8,128)S(1)}, u32[]{:S(2)}, u32[]{:S(2)}) %collective-permute-start.1) | collective-permute-done | bytes 131104 | tf_op jit(solution)/shard_map/ppermute | solution.py:347
  6.3 4.0 %collective-permute-done = f32[2,128,128]{2,1,0:T(8,128)S(1)} collective-permute-done((f32[2,128,128]{2,1,0:T(8,128)S(1)}, f32[2,128,128]{2,1,0:T(8,128)S(1)}, u32[]{:S(2)}, u32[]{:S(2)}) %collective-permute-start) | collective-permute-done | bytes 131104 | tf_op jit(solution)/shard_map/ppermute | solution.py:347
  10.4 0.1 collective-permute-start.3
  10.5 0.7 %collective-permute-start.2 = (f32[2,384,128]{2,1,0:T(8,128)S(1)}, f32[2,384,128]{2,1,0:T(8,128)S(1)}, u32[]{:S(2)}, u32[]{:S(2)}) collective-permute-start(f32[2,384,128]{2,1,0:T(8,128)S(1)} %pad_maximum_fusion.1.mid), channel_id=1, source_target_pairs={{1,2},{2,1},{3,4},{4,3},{5,6},{6,5},{7,8},{8,7},{9,10},{10,9},{11,... | collective-permute-start | bytes 1179656 | tf_op jit(solution)/shard_map/ppermute | solution.py:347
  11.2 0.1 add_and_fusion.parity
  11.2 0.8 %copy.11.dither = s32[4,2]{1,0:T(4,128)S(1)} copy(s32[4,2]{0,1:T(2,128)} %param.11) | data formatting | bytes 64 | tf_op args[4]
  12.0 1.0 %compare_convert_fusion = f32[4,128,128]{2,1,0:T(8,128)S(1)} fusion(s32[4,128,128]{2,1,0:T(8,128)} %param.8), kind=kLoop, calls=%fused_computation.3 | loop fusion | flops 131072 | bytes 524288 | tf_op jit(solution)/shard_map/convert_element_type | solution.py:363
  13.0 1.0 %pad_maximum_fusion.visits = f32[8,128,128]{2,1,0:T(8,128)S(1)} fusion(f32[4,128,128]{2,1,0:T(8,128)S(1)} %compare_convert_fusion, f32[4,128,128]{2,1,0:T(8,128)} %param.7), kind=kLoop, calls=%fused_computation | loop fusion | flops 131072 | bytes 1048576 | tf_op jit(solution)/shard_map/concatenate | solution.py:363
  14.0 0.0 collective-permute-done.3.side_b
  14.0 0.0 collective-permute-done.2.side_a
  14.0 0.0 copy-done
  14.0 0.0 copy-done.1
  14.0 18.1 %fit.1 = (f32[4,128,128]{2,1,0:T(8,128)S(1)}, f32[4,128,128]{2,1,0:T(8,128)S(1)}, f32[8,128]{1,0:T(8,128)S(1)}) custom-call(s32[4,2]{1,0:T(4,128)S(1)} %copy.11.dither, s32[4,12]{1,0:T(4,128)S(1)} %bitcast.5, s32[2]{0:T(128)S(1)} %add_and_fusion.parity, f32[2,384,128]{2,1,0:T(8,128)S(1)} %pad_maximum_fusion.1.mid, ...), custom_call_target="tpu_custom_call" | custom-call | tf_op jit(solution)/shard_map/fit/pallas_call | solution.py:321
  32.1 0.1 slice_reduce_fusion
  32.3 31.9 %all_to_all.6 = f32[32,1,4]{2,1,0:T(1,128)S(1)} all-to-all(f32[32,1,4]{2,1,0:T(1,128)S(1)} %broadcast_in_dim.8), channel_id=1, replica_groups=mesh['frow'=8,'fcol'=32] {'fcol'}, dimensions={0} | all-to-all | bytes 1024 | tf_op jit(solution)/shard_map/all_to_all | solution.py:353
  64.1 0.1 reduce_sum.9
  64.2 0.8 %rsqrt_multiply_fusion = f32[4,128,128]{2,1,0:T(8,128)} fusion(f32[4,128,128]{2,1,0:T(8,128)S(1)} %get-tuple-element.14, f32[4,128,128]{2,1,0:T(8,128)S(1)} %get-tuple-element.16, f32[4]{0:T(128)S(1)} %broadcast_multiply_fusion), kind=kLoop, calls=%fused_computation.2 | loop fusion | flops 196608 | bytes 786448 | tf_op jit(solution)/shard_map/mul | solution.py:372
  (3 shorter events, 0.0 us)
Async XLA Ops:
  0.0 14.0 %copy-start = (bf16[512,1536]{1,0:T(8,128)(2,1)S(1)}, bf16[512,1536]{1,0:T(8,128)(2,1)}, u32[]{:S(2)}) copy-start(bf16[512,1536]{1,0:T(8,128)(2,1)} %constant.22.clone.tables) | copy-start | bytes 4718596
  0.0 14.0 %copy-start.1 = (s32[4,1,1,12]{3,2,1,0:T(1,128)S(1)}, s32[4,1,1,12]{3,2,1,0:T(1,128)}, u32[]{:S(2)}) copy-start(s32[4,1,1,12]{3,2,1,0:T(1,128)} %param.12) | copy-start | bytes 580
  1.0 5.3 %collective-permute-start.1 = (f32[2,128,128]{2,1,0:T(8,128)S(1)}, f32[2,128,128]{2,1,0:T(8,128)S(1)}, u32[]{:S(2)}, u32[]{:S(2)}) collective-permute-start(f32[2,128,128]{2,1,0:T(8,128)S(1)} %pad_maximum_fusion.2), channel_id=1, source_target_pairs={{0,32},{32,0},{64,96},{96,64},{128,160},{160,128},{192,224},{224,1... | collective-permute-start | bytes 393224 | tf_op jit(solution)/shard_map/ppermute | solution.py:347
  2.6 7.7 %collective-permute-start = (f32[2,128,128]{2,1,0:T(8,128)S(1)}, f32[2,128,128]{2,1,0:T(8,128)S(1)}, u32[]{:S(2)}, u32[]{:S(2)}) collective-permute-start(f32[2,128,128]{2,1,0:T(8,128)S(1)} %pad_maximum_fusion.2), channel_id=1, source_target_pairs={{32,64},{64,32},{96,128},{128,96},{160,192},{192,160},{33,65},{65,... | collective-permute-start | bytes 393224 | tf_op jit(solution)/shard_map/ppermute | solution.py:347
  10.4 3.6 %collective-permute-start.3 = (f32[2,384,128]{2,1,0:T(8,128)S(1)}, f32[2,384,128]{2,1,0:T(8,128)S(1)}, u32[]{:S(2)}, u32[]{:S(2)}) collective-permute-start(f32[2,384,128]{2,1,0:T(8,128)S(1)} %pad_maximum_fusion.1.mid), channel_id=1, source_target_pairs={{0,1},{1,0},{2,3},{3,2},{4,5},{5,4},{6,7},{7,6},{8,9},{9,8},{10,11... | collective-permute-start | bytes 1179656 | tf_op jit(solution)/shard_map/ppermute | solution.py:347
  10.5 3.5 %collective-permute-start.2 = (f32[2,384,128]{2,1,0:T(8,128)S(1)}, f32[2,384,128]{2,1,0:T(8,128)S(1)}, u32[]{:S(2)}, u32[]{:S(2)}) collective-permute-start(f32[2,384,128]{2,1,0:T(8,128)S(1)} %pad_maximum_fusion.1.mid), channel_id=1, source_target_pairs={{1,2},{2,1},{3,4},{4,3},{5,6},{6,5},{7,8},{8,7},{9,10},{10,9},{11,... | collective-permute-start | bytes 1179656 | tf_op jit(solution)/shard_map/ppermute | solution.py:347

commit v4 on v3

--- a/solution.py
+++ b/solution.py
@@ -73,47 +73,34 @@
     return pltpu.roll(x, shift, 1)
 
 
-def body(dither, stamps, parity, mid, side_a, side_b, visits, tables,
-         diff_out, var_out, tot_out, planes, cbuf, sbuf, dbuf, gbuf, wbuf):
+def gather_planes(planes, parity, mid, side_a, side_b):
     row_a = pl.multiple_of(parity[0] * 256, 128)
     row_b = pl.multiple_of(256 - parity[0] * 256, 128)
-    for p in range(2):
-        for b, ref in ((1, mid), (2 * parity[1], side_a), (2 - 2 * parity[1], side_b)):
-            planes[p, b, pl.ds(row_a, 128), :] = ref[p, 0:128, :]
-            planes[p, b, 128:256, :] = ref[p, 128:256, :]
-            planes[p, b, pl.ds(row_b, 128), :] = ref[p, 256:384, :]
-            planes[p, b, 384:PROWS, :] = jnp.zeros((PROWS - 384, 128), F32)
-    lane = lax.broadcasted_iota(jnp.int32, (8, 128), 1)
-    sub = lax.broadcasted_iota(jnp.int32, (8, 128), 0)
-    lane1 = lane[0:1]
-
+    for b, ref in ((1, mid), (2 * parity[1], side_a), (2 - 2 * parity[1], side_b)):
+        planes[b, pl.ds(row_a, 128), :] = ref[0:128, :]
+        planes[b, 128:256, :] = ref[128:256, :]
+        planes[b, pl.ds(row_b, 128), :] = ref[256:384, :]
+        planes[b, 384:PROWS, :] = jnp.zeros((PROWS - 384, 128), F32)
+
+
+def basis_body(dither, parity, mid, side_a, side_b, visits, tables, dbuf, planes, cbuf, sbuf):
+    gather_planes(planes, parity, mid.at[0], side_a, side_b.at[0])
+    lane1 = lax.broadcasted_iota(jnp.int32, (1, 128), 1)
     windows = []
     for v in range(V):
-        dy = dither[v, 0]
-        dx = dither[v, 1]
-        row0 = DMAX + dy
-        col0 = DMAX + dx
+        row0 = DMAX + dither[v, 0]
+        col0 = DMAX + dither[v, 1]
         b0 = lax.shift_right_logical(col0, 7)
         s = jnp.bitwise_and(col0, 127)
         back = jnp.bitwise_and(128 - s, 127)
         last = jnp.minimum(b0 + 2, 2)
-        t0 = roll_lanes(planes[0, b0, pl.ds(row0, WROWS), :], back)
-        t1 = roll_lanes(planes[0, b0 + 1, pl.ds(row0, WROWS), :], back)
-        t2 = roll_lanes(planes[0, last, pl.ds(row0, WROWS), :], back)
+        t0 = roll_lanes(planes[b0, pl.ds(row0, WROWS), :], back)
+        t1 = roll_lanes(planes[b0 + 1, pl.ds(row0, WROWS), :], back)
+        t2 = roll_lanes(planes[last, pl.ds(row0, WROWS), :], back)
         keep = lane1 < 128 - s
         windows.append(
             jnp.concatenate([jnp.where(keep, t0, t1), jnp.where(keep, t1, t2)], axis=1).astype(BF)
         )
-        col1 = MARGIN + dx
-        b1 = lax.shift_right_logical(col1, 7)
-        s1 = jnp.bitwise_and(col1, 127)
-        back1 = jnp.bitwise_and(128 - s1, 127)
-        nxt = jnp.minimum(b1 + 1, 2)
-        q0 = roll_lanes(planes[1, b1, pl.ds(MARGIN + dy, TH), :], back1)
-        q1 = roll_lanes(planes[1, nxt, pl.ds(MARGIN + dy, TH), :], back1)
-        var = jnp.where(lane1 < 128 - s1, q0, q1)
-        var_out[v] = var
-        wbuf[v] = visits[V + v] / (0.25 + var)
         sbuf[:, v * TW : (v + 1) * TW] = visits[v].astype(BF)
 
     for v in range(V):
@@ -136,6 +123,26 @@
         return carry
 
     lax.fori_loop(0, TH // YB, row_block, 0)
+
+
+def fit_body(dither, stamps, parity, mid, side_a, side_b, visits, dbuf,
+             diff_out, var_out, tot_out, planes, gbuf, wbuf):
+    gather_planes(planes, parity, mid.at[1], side_a, side_b.at[1])
+    lane = lax.broadcasted_iota(jnp.int32, (8, 128), 1)
+    sub = lax.broadcasted_iota(jnp.int32, (8, 128), 0)
+    lane1 = lane[0:1]
+    for v in range(V):
+        row1 = MARGIN + dither[v, 0]
+        col1 = MARGIN + dither[v, 1]
+        b1 = lax.shift_right_logical(col1, 7)
+        s1 = jnp.bitwise_and(col1, 127)
+        back1 = jnp.bitwise_and(128 - s1, 127)
+        nxt = jnp.minimum(b1 + 1, 2)
+        q0 = roll_lanes(planes[b1, pl.ds(row1, TH), :], back1)
+        q1 = roll_lanes(planes[nxt, pl.ds(row1, TH), :], back1)
+        var = jnp.where(lane1 < 128 - s1, q0, q1)
+        var_out[v] = var
+        wbuf[v] = visits[V + v] / (0.25 + var)
 
     lanes32 = lax.broadcasted_iota(jnp.int32, (32, 128), 1)
     half_masks = [(lanes32 // 64 == h).astype(F32) for h in range(2)]
@@ -309,35 +316,55 @@
     )
 
 
-def fit_kernel(dither, stamps, parity, mid, side_a, side_b, visits):
+def table_array():
     table = kernel_table()
-    vmem = pl.BlockSpec(memory_space=pltpu.VMEM)
-    smem = pl.BlockSpec(memory_space=pltpu.SMEM)
     tables = np.zeros((512, F * TW), BF)
     tables[0:256] = column_matrix(table)
     rows = row_matrix(table)
     tables[256:512, 0:KDIM] = rows[0:256]
     tables[256:512, 640 : 640 + KDIM] = rows[256:512]
+    return jnp.asarray(tables)
+
+
+VMEM = pl.BlockSpec(memory_space=pltpu.VMEM)
+SMEM = pl.BlockSpec(memory_space=pltpu.SMEM)
+PARAMS = pltpu.CompilerParams(vmem_limit_bytes=16 * 1024 * 1024)
+
+
+def basis_kernel(dither, parity, mid, side_a, side_b, visits):
     return pl.pallas_call(
-        body,
+        basis_body,
+        out_shape=jax.ShapeDtypeStruct((TH * 32, V * TW), BF),
+        in_specs=[SMEM] * 2 + [VMEM] * 5,
+        out_specs=VMEM,
+        scratch_shapes=[
+            pltpu.VMEM((3, PROWS, 128), F32),
+            pltpu.VMEM((F, WROWS, V * TW), BF),
+            pltpu.VMEM((TH, V * TW), BF),
+        ],
+        compiler_params=PARAMS,
+        name="basis",
+    )(dither, parity, mid, side_a, side_b, visits, table_array())
+
+
+def fit_kernel(dither, stamps, parity, mid, side_a, side_b, visits, basis):
+    return pl.pallas_call(
+        fit_body,
         out_shape=(
             jax.ShapeDtypeStruct((V, TH, TW), F32),
             jax.ShapeDtypeStruct((V, TH, TW), F32),
             jax.ShapeDtypeStruct((8, 128), F32),
         ),
-        in_specs=[smem] * 3 + [vmem] * 5,
-        out_specs=(vmem, vmem, vmem),
+        in_specs=[SMEM] * 3 + [VMEM] * 5,
+        out_specs=(VMEM, VMEM, VMEM),
         scratch_shapes=[
-            pltpu.VMEM((2, 3, PROWS, 128), F32),
-            pltpu.VMEM((F, WROWS, V * TW), BF),
-            pltpu.VMEM((TH, V * TW), BF),
-            pltpu.VMEM((TH * 32, V * TW), BF),
+            pltpu.VMEM((3, PROWS, 128), F32),
             pltpu.VMEM((V, 4, 32, 128), F32),
             pltpu.VMEM((V, TH, TW), F32),
         ],
-        compiler_params=pltpu.CompilerParams(vmem_limit_bytes=20 * 1024 * 1024),
+        compiler_params=PARAMS,
         name="fit",
-    )(dither, stamps, parity, mid, side_a, side_b, visits, jnp.asarray(tables))
+    )(dither, stamps, parity, mid, side_a, side_b, visits, basis)
 
 
 def exchange(x, axis, first):
@@ -361,10 +388,12 @@
     mid = jnp.concatenate([rows_a, planes, rows_b], axis=1)
     mid, science, pixel_mask = lax.optimization_barrier((mid, science, pixel_mask))
     visits = jnp.concatenate([science, (pixel_mask == 0).astype(F32)], axis=0)
+    image_a = exchange(mid[0], "fcol", 1)
     side_b = exchange(mid, "fcol", 0)
-    side_a = exchange(mid, "fcol", 1)
+    var_a = exchange(mid[1], "fcol", 1)
+    basis = basis_kernel(dither, parity, mid, image_a, side_b, visits)
     diff, var, tot = fit_kernel(
-        dither, stamps.reshape(V, SMAX), parity, mid, side_a, side_b, visits
+        dither, stamps.reshape(V, SMAX), parity, mid, var_a, side_b, visits, basis
     )
     tot = strip_sum(tot[:V, 0])
     pixel_count = TH * TW * lax.axis_size("fcol")

time: 65.3 us -> 62 us (0.949)
  blocking collectives: 31.9 us -> 27.8 us
  waiting for transfers between devices: 5.13 us -> 4.29 us
  Pallas kernels: 18.1 us -> 18.9 us
  starting transfers between devices: 4.97 us -> 5.63 us
    all_to_all x1, blocking collectives: 31.9 us -> 27.8 us  [strip_sum(): return jnp.sum(lax.all_to_all(parts, 'fcol', 0, 0, tiled=True), axis=0)]
    ppermute x4 -> x5, waiting for transfers between devices: 5.13 us -> 4.29 us  [exchange(): return lax.ppermute(x, axis, pairs)]
    pallas_call x1 -> x2, Pallas kernels: 18.1 us -> 18.9 us  [the longest x1 13 us: fit_kernel(): pl.pallas_call(fit_body, out_shape=(jax.ShapeDtypeStruct((V, TH, TW), F32...]
    ppermute x4 -> x5, starting transfers between devices: 4.97 us -> 5.63 us  [exchange(): return lax.ppermute(x, axis, pairs)]
  transfers between devices with their start and end apart: 4 -> 5, of which waited for: 2 -> 2; matrix products, arithmetic and copies ran while one was open for 4% -> 5% of each run, Pallas kernels for 0% -> 10%
where the time goes in v4:
time: 62 us; the launch traced here: 61.7 us
  blocking collectives  27.8 us (45%)
  Pallas kernels  18.9 us (30%)
  starting transfers between devices  5.63 us (9%)
  waiting for transfers between devices  4.29 us (7%)
  other arithmetic  3.94 us (6%)
  local copies, waits for them, and re-layouts  0.94 us (2%)
    all_to_all x1, blocking collectives, strip_sum(): return jnp.sum(lax.all_to_all(parts, 'fcol', 0, 0, tiled=True), axis=0)  27.8 us
    pallas_call x1, Pallas kernels, fit_kernel(): pl.pallas_call(fit_body, out_shape=(jax.ShapeDtypeStruct((V, TH, TW), F32...  13 us
    pallas_call x1, Pallas kernels, basis_kernel(): pl.pallas_call(basis_body, out_shape=jax.ShapeDtypeStruct((TH * 32, V * T...  5.95 us
    ppermute x5, starting transfers between devices, exchange(): return lax.ppermute(x, axis, pairs)  5.63 us
    ppermute x5, waiting for transfers between devices, exchange(): return lax.ppermute(x, axis, pairs)  4.29 us
  transfers between devices with their start and end apart: 5, of which 2 were waited for; matrix products, arithmetic and copies ran while one was open for 5% of the time, Pallas kernels for 10%

profile of v4, /device:TPU:24, one launch (start us, length us, event | category | flops | bytes accessed | tf_op | source)
XLA Modules:
  0.0 61.7 jit_solution(3070028725740320299)
XLA Ops:
  0.0 0.0 copy-start
  0.0 1.0 %pad_maximum_fusion.2 = f32[2,128,128]{2,1,0:T(8,128)S(1)} fusion(f32[1,128,128]{2,1,0:T(8,128)} %bitcast.10, f32[1,128,128]{2,1,0:T(8,128)} %bitcast.11), kind=kLoop, calls=%fused_computation.6 | loop fusion | flops 32768 | bytes 262144 | tf_op jit(solution)/shard_map/stack | solution.py:385
  1.0 1.6 %collective-permute-start.1 = (f32[2,128,128]{2,1,0:T(8,128)S(1)}, f32[2,128,128]{2,1,0:T(8,128)S(1)}, u32[]{:S(2)}, u32[]{:S(2)}) collective-permute-start(f32[2,128,128]{2,1,0:T(8,128)S(1)} %pad_maximum_fusion.2), channel_id=1, source_target_pairs={{0,32},{32,0},{64,96},{96,64},{128,160},{160,128},{192,224},{224,1... | collective-permute-start | bytes 393224 | tf_op jit(solution)/shard_map/ppermute | solution.py:374
  2.6 2.6 %collective-permute-start = (f32[2,128,128]{2,1,0:T(8,128)S(1)}, f32[2,128,128]{2,1,0:T(8,128)S(1)}, u32[]{:S(2)}, u32[]{:S(2)}) collective-permute-start(f32[2,128,128]{2,1,0:T(8,128)S(1)} %pad_maximum_fusion.2), channel_id=1, source_target_pairs={{32,64},{64,32},{96,128},{128,96},{160,192},{192,160},{33,65},{65,... | collective-permute-start | bytes 393224 | tf_op jit(solution)/shard_map/ppermute | solution.py:374
  5.2 0.8 %copy.15.dither = s32[4,2]{1,0:T(4,128)S(1)} copy(s32[4,2]{0,1:T(2,128)} %param.11) | data formatting | bytes 64 | tf_op args[4]
  6.0 0.1 add_and_fusion.parity
  6.1 0.3 collective-permute-done.1
  6.3 4.0 %collective-permute-done = f32[2,128,128]{2,1,0:T(8,128)S(1)} collective-permute-done((f32[2,128,128]{2,1,0:T(8,128)S(1)}, f32[2,128,128]{2,1,0:T(8,128)S(1)}, u32[]{:S(2)}, u32[]{:S(2)}) %collective-permute-start) | collective-permute-done | bytes 131104 | tf_op jit(solution)/shard_map/ppermute | solution.py:374
  10.4 0.1 collective-permute-start.3
  10.5 0.7 %collective-permute-start.4 = (f32[384,128]{1,0:T(8,128)S(1)}, f32[384,128]{1,0:T(8,128)S(1)}, u32[]{:S(2)}, u32[]{:S(2)}) collective-permute-start(f32[384,128]{1,0:T(8,128)S(1)} %get-tuple-element.17), channel_id=1, source_target_pairs={{1,2},{2,1},{3,4},{4,3},{5,6},{6,5},{7,8},{8,7},{9,10},{10,9},{11,... | collective-permute-start | bytes 589832 | tf_op jit(solution)/shard_map/ppermute | solution.py:374
  11.2 0.7 %collective-permute-start.2 = (f32[384,128]{1,0:T(8,128)S(1)}, f32[384,128]{1,0:T(8,128)S(1)}, u32[]{:S(2)}, u32[]{:S(2)}) collective-permute-start(f32[384,128]{1,0:T(8,128)S(1)} %get-tuple-element.18), channel_id=1, source_target_pairs={{1,2},{2,1},{3,4},{4,3},{5,6},{6,5},{7,8},{8,7},{9,10},{10,9},{11,... | collective-permute-start | bytes 589832 | tf_op jit(solution)/shard_map/ppermute | solution.py:374
  11.9 1.0 %compare_convert_fusion = f32[4,128,128]{2,1,0:T(8,128)S(1)} fusion(s32[4,128,128]{2,1,0:T(8,128)} %param.8), kind=kLoop, calls=%fused_computation.3 | loop fusion | flops 131072 | bytes 524288 | tf_op jit(solution)/shard_map/convert_element_type | solution.py:390
  12.8 0.0 copy-start.1
  12.9 1.0 %pad_maximum_fusion.visits = f32[8,128,128]{2,1,0:T(8,128)S(1)} fusion(f32[4,128,128]{2,1,0:T(8,128)S(1)} %compare_convert_fusion, f32[4,128,128]{2,1,0:T(8,128)} %param.7), kind=kLoop, calls=%fused_computation | loop fusion | flops 131072 | bytes 1048576 | tf_op jit(solution)/shard_map/concatenate | solution.py:390
  13.8 0.0 collective-permute-done.4.side_a
  13.9 0.0 collective-permute-done.3.side_b
  13.9 0.0 copy-done
  13.9 6.0 %basis.1.dbuf = bf16[4096,512]{1,0:T(8,128)(2,1)S(1)} custom-call(s32[4,2]{1,0:T(4,128)S(1)} %copy.15.dither, s32[2]{0:T(128)S(1)} %add_and_fusion.parity, f32[2,384,128]{2,1,0:T(8,128)S(1)} %pad_maximum_fusion.1.mid, f32[384,128]{1,0:T(8,128)S(1)} %collective-permute-done.4.side_a, f32[2,384,128]{2,1,0:T(8,128)S(1)} %collective-permute-done.3.side_b, ...), custom_call_target="tpu_custom_call" | custom-call | tf_op jit(solution)/shard_map/basis/pallas_call | solution.py:335
  19.8 0.0 collective-permute-done.2.side_a
  19.8 0.0 copy-done.1
  19.9 13.0 %fit.1 = (f32[4,128,128]{2,1,0:T(8,128)S(1)}, f32[4,128,128]{2,1,0:T(8,128)S(1)}, f32[8,128]{1,0:T(8,128)S(1)}) custom-call(s32[4,2]{1,0:T(4,128)S(1)} %copy.15.dither, s32[4,12]{1,0:T(4,128)S(1)} %bitcast.9, s32[2]{0:T(128)S(1)} %add_and_fusion.parity, f32[2,384,128]{2,1,0:T(8,128)S(1)} %pad_maximum_fusion.1.mid, ...), custom_call_target="tpu_custom_call" | custom-call | tf_op jit(solution)/shard_map/fit/pallas_call | solution.py:351
  32.9 0.1 slice_reduce_fusion
  33.0 27.8 %all_to_all.6 = f32[32,1,4]{2,1,0:T(1,128)S(1)} all-to-all(f32[32,1,4]{2,1,0:T(1,128)S(1)} %broadcast_in_dim.8), channel_id=1, replica_groups=mesh['frow'=8,'fcol'=32] {'fcol'}, dimensions={0} | all-to-all | bytes 1024 | tf_op jit(solution)/shard_map/all_to_all | solution.py:380
  60.8 0.1 reduce_sum.9
  60.9 0.8 %rsqrt_multiply_fusion = f32[4,128,128]{2,1,0:T(8,128)} fusion(f32[4,128,128]{2,1,0:T(8,128)S(1)} %get-tuple-element.14, f32[4,128,128]{2,1,0:T(8,128)S(1)} %get-tuple-element.16, f32[4]{0:T(128)S(1)} %broadcast_multiply_fusion), kind=kLoop, calls=%fused_computation.2 | loop fusion | flops 196608 | bytes 786448 | tf_op jit(solution)/shard_map/mul | solution.py:401
  (4 shorter events, 0.1 us)
Async XLA Ops:
  0.0 13.9 %copy-start = (bf16[512,1536]{1,0:T(8,128)(2,1)S(1)}, bf16[512,1536]{1,0:T(8,128)(2,1)}, u32[]{:S(2)}) copy-start(bf16[512,1536]{1,0:T(8,128)(2,1)} %constant.22.clone.tables) | copy-start | bytes 4718596
  1.0 5.3 %collective-permute-start.1 = (f32[2,128,128]{2,1,0:T(8,128)S(1)}, f32[2,128,128]{2,1,0:T(8,128)S(1)}, u32[]{:S(2)}, u32[]{:S(2)}) collective-permute-start(f32[2,128,128]{2,1,0:T(8,128)S(1)} %pad_maximum_fusion.2), channel_id=1, source_target_pairs={{0,32},{32,0},{64,96},{96,64},{128,160},{160,128},{192,224},{224,1... | collective-permute-start | bytes 393224 | tf_op jit(solution)/shard_map/ppermute | solution.py:374
  2.6 7.7 %collective-permute-start = (f32[2,128,128]{2,1,0:T(8,128)S(1)}, f32[2,128,128]{2,1,0:T(8,128)S(1)}, u32[]{:S(2)}, u32[]{:S(2)}) collective-permute-start(f32[2,128,128]{2,1,0:T(8,128)S(1)} %pad_maximum_fusion.2), channel_id=1, source_target_pairs={{32,64},{64,32},{96,128},{128,96},{160,192},{192,160},{33,65},{65,... | collective-permute-start | bytes 393224 | tf_op jit(solution)/shard_map/ppermute | solution.py:374
  10.4 3.5 %collective-permute-start.3 = (f32[2,384,128]{2,1,0:T(8,128)S(1)}, f32[2,384,128]{2,1,0:T(8,128)S(1)}, u32[]{:S(2)}, u32[]{:S(2)}) collective-permute-start(f32[2,384,128]{2,1,0:T(8,128)S(1)} %pad_maximum_fusion.1.mid), channel_id=1, source_target_pairs={{0,1},{1,0},{2,3},{3,2},{4,5},{5,4},{6,7},{7,6},{8,9},{9,8},{10,11... | collective-permute-start | bytes 1179656 | tf_op jit(solution)/shard_map/ppermute | solution.py:374
  10.5 3.4 %collective-permute-start.4 = (f32[384,128]{1,0:T(8,128)S(1)}, f32[384,128]{1,0:T(8,128)S(1)}, u32[]{:S(2)}, u32[]{:S(2)}) collective-permute-start(f32[384,128]{1,0:T(8,128)S(1)} %get-tuple-element.17), channel_id=1, source_target_pairs={{1,2},{2,1},{3,4},{4,3},{5,6},{6,5},{7,8},{8,7},{9,10},{10,9},{11,... | collective-permute-start | bytes 589832 | tf_op jit(solution)/shard_map/ppermute | solution.py:374
  11.2 8.7 %collective-permute-start.2 = (f32[384,128]{1,0:T(8,128)S(1)}, f32[384,128]{1,0:T(8,128)S(1)}, u32[]{:S(2)}, u32[]{:S(2)}) collective-permute-start(f32[384,128]{1,0:T(8,128)S(1)} %get-tuple-element.18), channel_id=1, source_target_pairs={{1,2},{2,1},{3,4},{4,3},{5,6},{6,5},{7,8},{8,7},{9,10},{10,9},{11,... | collective-permute-start | bytes 589832 | tf_op jit(solution)/shard_map/ppermute | solution.py:374
  12.8 7.0 %copy-start.1 = (s32[4,1,1,12]{3,2,1,0:T(1,128)S(1)}, s32[4,1,1,12]{3,2,1,0:T(1,128)}, u32[]{:S(2)}) copy-start(s32[4,1,1,12]{3,2,1,0:T(1,128)} %param.12) | copy-start | bytes 580

commit v5 on v4

--- a/solution.py
+++ b/solution.py
@@ -122,7 +122,7 @@
         dbuf[pl.ds(pl.multiple_of(yb * (YB * 32), YB * 32), YB * 32), :] = out
         return carry
 
-    lax.fori_loop(0, TH // YB, row_block, 0)
+    lax.fori_loop(0, TH // YB, row_block, 0, unroll=2)
 
 
 def fit_body(dither, stamps, parity, mid, side_a, side_b, visits, dbuf,
@@ -169,7 +169,7 @@
             gbuf[v, i] = jnp.concatenate([acc[:32], acc[32:]], axis=1)
             return carry
 
-        lax.fori_loop(0, 4, gram_row, 0)
+        lax.fori_loop(0, 4, gram_row, 0, unroll=2)
 
     group = lane // 32
     xs = (group.astype(F32) - 1.5) * 0.5

time: 62 us -> 59.4 us (0.958)
  Pallas kernels: 18.9 us -> 16.4 us
    pallas_call x1, Pallas kernels: 13 us -> 11.1 us  [fit_kernel(): pl.pallas_call(fit_body, out_shape=(jax.ShapeDtypeStruct((V, TH, TW), F32...]
    pallas_call x1, Pallas kernels: 5.95 us -> 5.27 us  [basis_kernel(): pl.pallas_call(basis_body, out_shape=jax.ShapeDtypeStruct((TH * 32, V * T...]
  transfers between devices with their start and end apart: 5 -> 5, of which waited for: 2 -> 2; matrix products, arithmetic and copies ran while one was open for 5% -> 5% of each run, Pallas kernels for 10% -> 9%
where the time goes in v5:
time: 59.4 us; the launch traced here: 59.1 us
  blocking collectives  27.8 us (47%)
  Pallas kernels  16.4 us (28%)
  starting transfers between devices  5.63 us (9%)
  waiting for transfers between devices  4.29 us (7%)
  other arithmetic  3.94 us (7%)
  local copies, waits for them, and re-layouts  0.94 us (2%)
    all_to_all x1, blocking collectives, strip_sum(): return jnp.sum(lax.all_to_all(parts, 'fcol', 0, 0, tiled=True), axis=0)  27.8 us
    pallas_call x1, Pallas kernels, fit_kernel(): pl.pallas_call(fit_body, out_shape=(jax.ShapeDtypeStruct((V, TH, TW), F32...  11.1 us
    ppermute x5, starting transfers between devices, exchange(): return lax.ppermute(x, axis, pairs)  5.63 us
    pallas_call x1, Pallas kernels, basis_kernel(): pl.pallas_call(basis_body, out_shape=jax.ShapeDtypeStruct((TH * 32, V * T...  5.27 us
    ppermute x5, waiting for transfers between devices, exchange(): return lax.ppermute(x, axis, pairs)  4.29 us
  transfers between devices with their start and end apart: 5, of which 2 were waited for; matrix products, arithmetic and copies ran while one was open for 5% of the time, Pallas kernels for 9%

profile of v5, /device:TPU:24, one launch (start us, length us, event | category | flops | bytes accessed | tf_op | source)
XLA Modules:
  0.0 59.1 jit_solution(5295179027768649607)
XLA Ops:
  0.0 0.0 copy-start
  0.0 1.0 %pad_maximum_fusion.2 = f32[2,128,128]{2,1,0:T(8,128)S(1)} fusion(f32[1,128,128]{2,1,0:T(8,128)} %bitcast.10, f32[1,128,128]{2,1,0:T(8,128)} %bitcast.11), kind=kLoop, calls=%fused_computation.6 | loop fusion | flops 32768 | bytes 262144 | tf_op jit(solution)/shard_map/stack | solution.py:385
  1.0 1.6 %collective-permute-start.1 = (f32[2,128,128]{2,1,0:T(8,128)S(1)}, f32[2,128,128]{2,1,0:T(8,128)S(1)}, u32[]{:S(2)}, u32[]{:S(2)}) collective-permute-start(f32[2,128,128]{2,1,0:T(8,128)S(1)} %pad_maximum_fusion.2), channel_id=1, source_target_pairs={{0,32},{32,0},{64,96},{96,64},{128,160},{160,128},{192,224},{224,1... | collective-permute-start | bytes 393224 | tf_op jit(solution)/shard_map/ppermute | solution.py:374
  2.6 2.6 %collective-permute-start = (f32[2,128,128]{2,1,0:T(8,128)S(1)}, f32[2,128,128]{2,1,0:T(8,128)S(1)}, u32[]{:S(2)}, u32[]{:S(2)}) collective-permute-start(f32[2,128,128]{2,1,0:T(8,128)S(1)} %pad_maximum_fusion.2), channel_id=1, source_target_pairs={{32,64},{64,32},{96,128},{128,96},{160,192},{192,160},{33,65},{65,... | collective-permute-start | bytes 393224 | tf_op jit(solution)/shard_map/ppermute | solution.py:374
  5.2 0.8 %copy.15.dither = s32[4,2]{1,0:T(4,128)S(1)} copy(s32[4,2]{0,1:T(2,128)} %param.11) | data formatting | bytes 64 | tf_op args[4]
  6.0 0.1 add_and_fusion.parity
  6.1 0.3 collective-permute-done.1
  6.3 4.0 %collective-permute-done = f32[2,128,128]{2,1,0:T(8,128)S(1)} collective-permute-done((f32[2,128,128]{2,1,0:T(8,128)S(1)}, f32[2,128,128]{2,1,0:T(8,128)S(1)}, u32[]{:S(2)}, u32[]{:S(2)}) %collective-permute-start) | collective-permute-done | bytes 131104 | tf_op jit(solution)/shard_map/ppermute | solution.py:374
  10.4 0.1 collective-permute-start.3
  10.5 0.7 %collective-permute-start.4 = (f32[384,128]{1,0:T(8,128)S(1)}, f32[384,128]{1,0:T(8,128)S(1)}, u32[]{:S(2)}, u32[]{:S(2)}) collective-permute-start(f32[384,128]{1,0:T(8,128)S(1)} %get-tuple-element.17), channel_id=1, source_target_pairs={{1,2},{2,1},{3,4},{4,3},{5,6},{6,5},{7,8},{8,7},{9,10},{10,9},{11,... | collective-permute-start | bytes 589832 | tf_op jit(solution)/shard_map/ppermute | solution.py:374
  11.2 0.7 %collective-permute-start.2 = (f32[384,128]{1,0:T(8,128)S(1)}, f32[384,128]{1,0:T(8,128)S(1)}, u32[]{:S(2)}, u32[]{:S(2)}) collective-permute-start(f32[384,128]{1,0:T(8,128)S(1)} %get-tuple-element.18), channel_id=1, source_target_pairs={{1,2},{2,1},{3,4},{4,3},{5,6},{6,5},{7,8},{8,7},{9,10},{10,9},{11,... | collective-permute-start | bytes 589832 | tf_op jit(solution)/shard_map/ppermute | solution.py:374
  11.9 1.0 %compare_convert_fusion = f32[4,128,128]{2,1,0:T(8,128)S(1)} fusion(s32[4,128,128]{2,1,0:T(8,128)} %param.8), kind=kLoop, calls=%fused_computation.3 | loop fusion | flops 131072 | bytes 524288 | tf_op jit(solution)/shard_map/convert_element_type | solution.py:390
  12.8 0.0 copy-start.1
  12.9 1.0 %pad_maximum_fusion.visits = f32[8,128,128]{2,1,0:T(8,128)S(1)} fusion(f32[4,128,128]{2,1,0:T(8,128)S(1)} %compare_convert_fusion, f32[4,128,128]{2,1,0:T(8,128)} %param.7), kind=kLoop, calls=%fused_computation | loop fusion | flops 131072 | bytes 1048576 | tf_op jit(solution)/shard_map/concatenate | solution.py:390
  13.8 0.0 collective-permute-done.4.side_a
  13.9 0.0 collective-permute-done.3.side_b
  13.9 0.0 copy-done
  13.9 5.3 %basis.1.dbuf = bf16[4096,512]{1,0:T(8,128)(2,1)S(1)} custom-call(s32[4,2]{1,0:T(4,128)S(1)} %copy.15.dither, s32[2]{0:T(128)S(1)} %add_and_fusion.parity, f32[2,384,128]{2,1,0:T(8,128)S(1)} %pad_maximum_fusion.1.mid, f32[384,128]{1,0:T(8,128)S(1)} %collective-permute-done.4.side_a, f32[2,384,128]{2,1,0:T(8,128)S(1)} %collective-permute-done.3.side_b, ...), custom_call_target="tpu_custom_call" | custom-call | tf_op jit(solution)/shard_map/basis/pallas_call | solution.py:335
  19.2 0.0 collective-permute-done.2.side_a
  19.2 0.0 copy-done.1
  19.2 11.1 %fit.1 = (f32[4,128,128]{2,1,0:T(8,128)S(1)}, f32[4,128,128]{2,1,0:T(8,128)S(1)}, f32[8,128]{1,0:T(8,128)S(1)}) custom-call(s32[4,2]{1,0:T(4,128)S(1)} %copy.15.dither, s32[4,12]{1,0:T(4,128)S(1)} %bitcast.9, s32[2]{0:T(128)S(1)} %add_and_fusion.parity, f32[2,384,128]{2,1,0:T(8,128)S(1)} %pad_maximum_fusion.1.mid, ...), custom_call_target="tpu_custom_call" | custom-call | tf_op jit(solution)/shard_map/fit/pallas_call | solution.py:351
  30.3 0.1 slice_reduce_fusion
  30.4 27.8 %all_to_all.6 = f32[32,1,4]{2,1,0:T(1,128)S(1)} all-to-all(f32[32,1,4]{2,1,0:T(1,128)S(1)} %broadcast_in_dim.8), channel_id=1, replica_groups=mesh['frow'=8,'fcol'=32] {'fcol'}, dimensions={0} | all-to-all | bytes 1024 | tf_op jit(solution)/shard_map/all_to_all | solution.py:380
  58.2 0.1 reduce_sum.9
  58.3 0.8 %rsqrt_multiply_fusion = f32[4,128,128]{2,1,0:T(8,128)} fusion(f32[4,128,128]{2,1,0:T(8,128)S(1)} %get-tuple-element.14, f32[4,128,128]{2,1,0:T(8,128)S(1)} %get-tuple-element.16, f32[4]{0:T(128)S(1)} %broadcast_multiply_fusion), kind=kLoop, calls=%fused_computation.2 | loop fusion | flops 196608 | bytes 786448 | tf_op jit(solution)/shard_map/mul | solution.py:401
  (4 shorter events, 0.1 us)
Async XLA Ops:
  0.0 13.9 %copy-start = (bf16[512,1536]{1,0:T(8,128)(2,1)S(1)}, bf16[512,1536]{1,0:T(8,128)(2,1)}, u32[]{:S(2)}) copy-start(bf16[512,1536]{1,0:T(8,128)(2,1)} %constant.22.clone.tables) | copy-start | bytes 4718596
  1.0 5.3 %collective-permute-start.1 = (f32[2,128,128]{2,1,0:T(8,128)S(1)}, f32[2,128,128]{2,1,0:T(8,128)S(1)}, u32[]{:S(2)}, u32[]{:S(2)}) collective-permute-start(f32[2,128,128]{2,1,0:T(8,128)S(1)} %pad_maximum_fusion.2), channel_id=1, source_target_pairs={{0,32},{32,0},{64,96},{96,64},{128,160},{160,128},{192,224},{224,1... | collective-permute-start | bytes 393224 | tf_op jit(solution)/shard_map/ppermute | solution.py:374
  2.6 7.7 %collective-permute-start = (f32[2,128,128]{2,1,0:T(8,128)S(1)}, f32[2,128,128]{2,1,0:T(8,128)S(1)}, u32[]{:S(2)}, u32[]{:S(2)}) collective-permute-start(f32[2,128,128]{2,1,0:T(8,128)S(1)} %pad_maximum_fusion.2), channel_id=1, source_target_pairs={{32,64},{64,32},{96,128},{128,96},{160,192},{192,160},{33,65},{65,... | collective-permute-start | bytes 393224 | tf_op jit(solution)/shard_map/ppermute | solution.py:374
  10.4 3.5 %collective-permute-start.3 = (f32[2,384,128]{2,1,0:T(8,128)S(1)}, f32[2,384,128]{2,1,0:T(8,128)S(1)}, u32[]{:S(2)}, u32[]{:S(2)}) collective-permute-start(f32[2,384,128]{2,1,0:T(8,128)S(1)} %pad_maximum_fusion.1.mid), channel_id=1, source_target_pairs={{0,1},{1,0},{2,3},{3,2},{4,5},{5,4},{6,7},{7,6},{8,9},{9,8},{10,11... | collective-permute-start | bytes 1179656 | tf_op jit(solution)/shard_map/ppermute | solution.py:374
  10.5 3.4 %collective-permute-start.4 = (f32[384,128]{1,0:T(8,128)S(1)}, f32[384,128]{1,0:T(8,128)S(1)}, u32[]{:S(2)}, u32[]{:S(2)}) collective-permute-start(f32[384,128]{1,0:T(8,128)S(1)} %get-tuple-element.17), channel_id=1, source_target_pairs={{1,2},{2,1},{3,4},{4,3},{5,6},{6,5},{7,8},{8,7},{9,10},{10,9},{11,... | collective-permute-start | bytes 589832 | tf_op jit(solution)/shard_map/ppermute | solution.py:374
  11.2 8.0 %collective-permute-start.2 = (f32[384,128]{1,0:T(8,128)S(1)}, f32[384,128]{1,0:T(8,128)S(1)}, u32[]{:S(2)}, u32[]{:S(2)}) collective-permute-start(f32[384,128]{1,0:T(8,128)S(1)} %get-tuple-element.18), channel_id=1, source_target_pairs={{1,2},{2,1},{3,4},{4,3},{5,6},{6,5},{7,8},{8,7},{9,10},{10,9},{11,... | collective-permute-start | bytes 589832 | tf_op jit(solution)/shard_map/ppermute | solution.py:374
  12.8 6.3 %copy-start.1 = (s32[4,1,1,12]{3,2,1,0:T(1,128)S(1)}, s32[4,1,1,12]{3,2,1,0:T(1,128)}, u32[]{:S(2)}) copy-start(s32[4,1,1,12]{3,2,1,0:T(1,128)} %param.12) | copy-start | bytes 580

commit v6 on v5

--- a/solution.py
+++ b/solution.py
@@ -122,7 +122,7 @@
         dbuf[pl.ds(pl.multiple_of(yb * (YB * 32), YB * 32), YB * 32), :] = out
         return carry
 
-    lax.fori_loop(0, TH // YB, row_block, 0, unroll=2)
+    lax.fori_loop(0, TH // YB, row_block, 0, unroll=4)
 
 
 def fit_body(dither, stamps, parity, mid, side_a, side_b, visits, dbuf,
@@ -169,7 +169,7 @@
             gbuf[v, i] = jnp.concatenate([acc[:32], acc[32:]], axis=1)
             return carry
 
-        lax.fori_loop(0, 4, gram_row, 0, unroll=2)
+        lax.fori_loop(0, 4, gram_row, 0, unroll=4)
 
     group = lane // 32
     xs = (group.astype(F32) - 1.5) * 0.5

time: 59.4 us -> 56.9 us (0.958)
  Pallas kernels: 16.4 us -> 13.9 us
    pallas_call x1, Pallas kernels: 11.1 us -> 8.91 us  [fit_kernel(): pl.pallas_call(fit_body, out_shape=(jax.ShapeDtypeStruct((V, TH, TW), F32...]
where the time goes in v6:
time: 56.9 us; the launch traced here: 56.6 us
  blocking collectives  27.8 us (49%)
  Pallas kernels  13.9 us (24%)
  starting transfers between devices  5.63 us (10%)
  waiting for transfers between devices  4.29 us (8%)
  other arithmetic  3.94 us (7%)
  local copies, waits for them, and re-layouts  0.94 us (2%)
    all_to_all x1, blocking collectives, strip_sum(): return jnp.sum(lax.all_to_all(parts, 'fcol', 0, 0, tiled=True), axis=0)  27.8 us
    pallas_call x1, Pallas kernels, fit_kernel(): pl.pallas_call(fit_body, out_shape=(jax.ShapeDtypeStruct((V, TH, TW), F32...  8.91 us
    ppermute x5, starting transfers between devices, exchange(): return lax.ppermute(x, axis, pairs)  5.63 us
    pallas_call x1, Pallas kernels, basis_kernel(): pl.pallas_call(basis_body, out_shape=jax.ShapeDtypeStruct((TH * 32, V * T...  4.95 us
    ppermute x5, waiting for transfers between devices, exchange(): return lax.ppermute(x, axis, pairs)  4.29 us
  transfers between devices with their start and end apart: 5, of which 2 were waited for; matrix products, arithmetic and copies ran while one was open for 5% of the time, Pallas kernels for 9%

profile of v6, /device:TPU:24, one launch (start us, length us, event | category | flops | bytes accessed | tf_op | source)
XLA Modules:
  0.0 56.6 jit_solution(638426016893561996)
XLA Ops:
  0.0 0.0 copy-start
  0.0 1.0 %pad_maximum_fusion.2 = f32[2,128,128]{2,1,0:T(8,128)S(1)} fusion(f32[1,128,128]{2,1,0:T(8,128)} %bitcast.10, f32[1,128,128]{2,1,0:T(8,128)} %bitcast.11), kind=kLoop, calls=%fused_computation.6 | loop fusion | flops 32768 | bytes 262144 | tf_op jit(solution)/shard_map/stack | solution.py:385
  1.0 1.6 %collective-permute-start.1 = (f32[2,128,128]{2,1,0:T(8,128)S(1)}, f32[2,128,128]{2,1,0:T(8,128)S(1)}, u32[]{:S(2)}, u32[]{:S(2)}) collective-permute-start(f32[2,128,128]{2,1,0:T(8,128)S(1)} %pad_maximum_fusion.2), channel_id=1, source_target_pairs={{0,32},{32,0},{64,96},{96,64},{128,160},{160,128},{192,224},{224,1... | collective-permute-start | bytes 393224 | tf_op jit(solution)/shard_map/ppermute | solution.py:374
  2.6 2.6 %collective-permute-start = (f32[2,128,128]{2,1,0:T(8,128)S(1)}, f32[2,128,128]{2,1,0:T(8,128)S(1)}, u32[]{:S(2)}, u32[]{:S(2)}) collective-permute-start(f32[2,128,128]{2,1,0:T(8,128)S(1)} %pad_maximum_fusion.2), channel_id=1, source_target_pairs={{32,64},{64,32},{96,128},{128,96},{160,192},{192,160},{33,65},{65,... | collective-permute-start | bytes 393224 | tf_op jit(solution)/shard_map/ppermute | solution.py:374
  5.2 0.8 %copy.15.dither = s32[4,2]{1,0:T(4,128)S(1)} copy(s32[4,2]{0,1:T(2,128)} %param.11) | data formatting | bytes 64 | tf_op args[4]
  6.0 0.1 add_and_fusion.parity
  6.1 0.3 collective-permute-done.1
  6.3 4.0 %collective-permute-done = f32[2,128,128]{2,1,0:T(8,128)S(1)} collective-permute-done((f32[2,128,128]{2,1,0:T(8,128)S(1)}, f32[2,128,128]{2,1,0:T(8,128)S(1)}, u32[]{:S(2)}, u32[]{:S(2)}) %collective-permute-start) | collective-permute-done | bytes 131104 | tf_op jit(solution)/shard_map/ppermute | solution.py:374
  10.4 0.1 collective-permute-start.3
  10.5 0.7 %collective-permute-start.4 = (f32[384,128]{1,0:T(8,128)S(1)}, f32[384,128]{1,0:T(8,128)S(1)}, u32[]{:S(2)}, u32[]{:S(2)}) collective-permute-start(f32[384,128]{1,0:T(8,128)S(1)} %get-tuple-element.17), channel_id=1, source_target_pairs={{1,2},{2,1},{3,4},{4,3},{5,6},{6,5},{7,8},{8,7},{9,10},{10,9},{11,... | collective-permute-start | bytes 589832 | tf_op jit(solution)/shard_map/ppermute | solution.py:374
  11.2 0.7 %collective-permute-start.2 = (f32[384,128]{1,0:T(8,128)S(1)}, f32[384,128]{1,0:T(8,128)S(1)}, u32[]{:S(2)}, u32[]{:S(2)}) collective-permute-start(f32[384,128]{1,0:T(8,128)S(1)} %get-tuple-element.18), channel_id=1, source_target_pairs={{1,2},{2,1},{3,4},{4,3},{5,6},{6,5},{7,8},{8,7},{9,10},{10,9},{11,... | collective-permute-start | bytes 589832 | tf_op jit(solution)/shard_map/ppermute | solution.py:374
  11.9 1.0 %compare_convert_fusion = f32[4,128,128]{2,1,0:T(8,128)S(1)} fusion(s32[4,128,128]{2,1,0:T(8,128)} %param.8), kind=kLoop, calls=%fused_computation.3 | loop fusion | flops 131072 | bytes 524288 | tf_op jit(solution)/shard_map/convert_element_type | solution.py:390
  12.8 0.0 copy-start.1
  12.9 1.0 %pad_maximum_fusion.visits = f32[8,128,128]{2,1,0:T(8,128)S(1)} fusion(f32[4,128,128]{2,1,0:T(8,128)S(1)} %compare_convert_fusion, f32[4,128,128]{2,1,0:T(8,128)} %param.7), kind=kLoop, calls=%fused_computation | loop fusion | flops 131072 | bytes 1048576 | tf_op jit(solution)/shard_map/concatenate | solution.py:390
  13.8 0.0 collective-permute-done.4.side_a
  13.9 0.0 collective-permute-done.3.side_b
  13.9 0.0 copy-done
  13.9 4.9 %basis.1.dbuf = bf16[4096,512]{1,0:T(8,128)(2,1)S(1)} custom-call(s32[4,2]{1,0:T(4,128)S(1)} %copy.15.dither, s32[2]{0:T(128)S(1)} %add_and_fusion.parity, f32[2,384,128]{2,1,0:T(8,128)S(1)} %pad_maximum_fusion.1.mid, f32[384,128]{1,0:T(8,128)S(1)} %collective-permute-done.4.side_a, f32[2,384,128]{2,1,0:T(8,128)S(1)} %collective-permute-done.3.side_b, ...), custom_call_target="tpu_custom_call" | custom-call | tf_op jit(solution)/shard_map/basis/pallas_call | solution.py:335
  18.8 0.0 collective-permute-done.2.side_a
  18.8 0.0 copy-done.1
  18.9 8.9 %fit.1 = (f32[4,128,128]{2,1,0:T(8,128)S(1)}, f32[4,128,128]{2,1,0:T(8,128)S(1)}, f32[8,128]{1,0:T(8,128)S(1)}) custom-call(s32[4,2]{1,0:T(4,128)S(1)} %copy.15.dither, s32[4,12]{1,0:T(4,128)S(1)} %bitcast.9, s32[2]{0:T(128)S(1)} %add_and_fusion.parity, f32[2,384,128]{2,1,0:T(8,128)S(1)} %pad_maximum_fusion.1.mid, ...), custom_call_target="tpu_custom_call" | custom-call | tf_op jit(solution)/shard_map/fit/pallas_call | solution.py:351
  27.8 0.1 slice_reduce_fusion
  27.9 27.8 %all_to_all.6 = f32[32,1,4]{2,1,0:T(1,128)S(1)} all-to-all(f32[32,1,4]{2,1,0:T(1,128)S(1)} %broadcast_in_dim.8), channel_id=1, replica_groups=mesh['frow'=8,'fcol'=32] {'fcol'}, dimensions={0} | all-to-all | bytes 1024 | tf_op jit(solution)/shard_map/all_to_all | solution.py:380
  55.7 0.1 reduce_sum.9
  55.8 0.8 %rsqrt_multiply_fusion = f32[4,128,128]{2,1,0:T(8,128)} fusion(f32[4,128,128]{2,1,0:T(8,128)S(1)} %get-tuple-element.14, f32[4,128,128]{2,1,0:T(8,128)S(1)} %get-tuple-element.16, f32[4]{0:T(128)S(1)} %broadcast_multiply_fusion), kind=kLoop, calls=%fused_computation.2 | loop fusion | flops 196608 | bytes 786448 | tf_op jit(solution)/shard_map/mul | solution.py:401
  (4 shorter events, 0.1 us)
Async XLA Ops:
  0.0 13.9 %copy-start = (bf16[512,1536]{1,0:T(8,128)(2,1)S(1)}, bf16[512,1536]{1,0:T(8,128)(2,1)}, u32[]{:S(2)}) copy-start(bf16[512,1536]{1,0:T(8,128)(2,1)} %constant.22.clone.tables) | copy-start | bytes 4718596
  1.0 5.3 %collective-permute-start.1 = (f32[2,128,128]{2,1,0:T(8,128)S(1)}, f32[2,128,128]{2,1,0:T(8,128)S(1)}, u32[]{:S(2)}, u32[]{:S(2)}) collective-permute-start(f32[2,128,128]{2,1,0:T(8,128)S(1)} %pad_maximum_fusion.2), channel_id=1, source_target_pairs={{0,32},{32,0},{64,96},{96,64},{128,160},{160,128},{192,224},{224,1... | collective-permute-start | bytes 393224 | tf_op jit(solution)/shard_map/ppermute | solution.py:374
  2.6 7.7 %collective-permute-start = (f32[2,128,128]{2,1,0:T(8,128)S(1)}, f32[2,128,128]{2,1,0:T(8,128)S(1)}, u32[]{:S(2)}, u32[]{:S(2)}) collective-permute-start(f32[2,128,128]{2,1,0:T(8,128)S(1)} %pad_maximum_fusion.2), channel_id=1, source_target_pairs={{32,64},{64,32},{96,128},{128,96},{160,192},{192,160},{33,65},{65,... | collective-permute-start | bytes 393224 | tf_op jit(solution)/shard_map/ppermute | solution.py:374
  10.4 3.5 %collective-permute-start.3 = (f32[2,384,128]{2,1,0:T(8,128)S(1)}, f32[2,384,128]{2,1,0:T(8,128)S(1)}, u32[]{:S(2)}, u32[]{:S(2)}) collective-permute-start(f32[2,384,128]{2,1,0:T(8,128)S(1)} %pad_maximum_fusion.1.mid), channel_id=1, source_target_pairs={{0,1},{1,0},{2,3},{3,2},{4,5},{5,4},{6,7},{7,6},{8,9},{9,8},{10,11... | collective-permute-start | bytes 1179656 | tf_op jit(solution)/shard_map/ppermute | solution.py:374
  10.5 3.4 %collective-permute-start.4 = (f32[384,128]{1,0:T(8,128)S(1)}, f32[384,128]{1,0:T(8,128)S(1)}, u32[]{:S(2)}, u32[]{:S(2)}) collective-permute-start(f32[384,128]{1,0:T(8,128)S(1)} %get-tuple-element.17), channel_id=1, source_target_pairs={{1,2},{2,1},{3,4},{4,3},{5,6},{6,5},{7,8},{8,7},{9,10},{10,9},{11,... | collective-permute-start | bytes 589832 | tf_op jit(solution)/shard_map/ppermute | solution.py:374
  11.2 7.7 %collective-permute-start.2 = (f32[384,128]{1,0:T(8,128)S(1)}, f32[384,128]{1,0:T(8,128)S(1)}, u32[]{:S(2)}, u32[]{:S(2)}) collective-permute-start(f32[384,128]{1,0:T(8,128)S(1)} %get-tuple-element.18), channel_id=1, source_target_pairs={{1,2},{2,1},{3,4},{4,3},{5,6},{6,5},{7,8},{8,7},{9,10},{10,9},{11,... | collective-permute-start | bytes 589832 | tf_op jit(solution)/shard_map/ppermute | solution.py:374
  12.8 6.0 %copy-start.1 = (s32[4,1,1,12]{3,2,1,0:T(1,128)S(1)}, s32[4,1,1,12]{3,2,1,0:T(1,128)}, u32[]{:S(2)}) copy-start(s32[4,1,1,12]{3,2,1,0:T(1,128)} %param.12) | copy-start | bytes 580
